TPU v7x, 32 devices: a whole 2x2x4 slice. The times are simulated.
32 devices in a mesh: gx: 4 (over y, x), gy: 8 (over z, core).
Axes of the slice: x: 2, y: 2, z: 4, core: 2. Of those that a mesh axis runs over, the one named last changes fastest.
Arguments:
- a_blocks: bfloat16 [16, 16, 5, 192, 192], P('gx', 'gy'), may hold values from -0.4375 to 0.4375
- a_codes: int32 [16, 16, 5], P('gx', 'gy'), may hold values from 0 to 9, as said below
- p_blocks: bfloat16 [16, 16, 3, 12, 192], P('gx', 'gy'), may hold values from -0.875 to 0.875
- p_codes: int32 [16, 16, 3], P('gx', 'gy'), may hold values from 0 to 5, as said below
Outputs:
- coarse: float32 [16, 16, 12, 588], P('gx', 'gy')
Inputs may be any that keep to these rules, and one draw needn't show every extreme that they name: `a_codes`: slot 0 is 4 (the aggregate itself); the other slots of one aggregate hold distinct codes or 9; some aggregates have every slot live. `p_codes`: slot 0 is 0 (the aggregate itself); the other slots of one aggregate hold distinct codes of 1 to 4 or 5; some aggregates have every slot live.
All inputs are finite; a program needn't handle non-finite values.
Results may differ from a plain program's by a relative error of at most 0.0029.
Values may be sent and summed in bfloat16 or wider, within the bound.
No kernel may reach another device: no remote copies, remote signals or barrier semaphores. Data moves between devices by JAX's collectives and lax.ppermute only.
A program may use at most 64 MiB of HBM per device.

v0:
```python
import jax
import jax.numpy as jnp
from jax import lax
from jax.experimental import pallas as pl
from jax.experimental.pallas import tpu as pltpu
from jax.sharding import PartitionSpec as P

face_steps = ((0, 0), (-1, 0), (1, 0), (0, -1), (0, 1))
ROWS = 16
NT = (((1,), (1,)), ((), ()))
AXES = ("gx", "gy")


def exchange_pairs(count_x, count_y):
    spot = lambda x, y: x * count_y + y
    result = []
    for parity in (0, 1):
        pairs = []
        for x in range(count_x):
            other = x + 1 if (x % 2 == parity) else x - 1
            for y in range(count_y):
                inside = 0 <= other < count_x
                pairs.append((spot(x, y), spot(other, y) if inside else spot(x, y ^ 1)))
        result.append(pairs)
    for parity in (0, 1):
        pairs = []
        for y in range(count_y):
            other = y + 1 if (y % 2 == parity) else y - 1
            for x in range(count_x):
                inside = 0 <= other < count_y
                pairs.append((spot(x, y), spot(x, other) if inside else spot(x ^ 1, y)))
        result.append(pairs)
    return result


def place(axis):
    index = lax.axis_index(axis)
    even = lax.rem(index, 2) == 0
    return index, even


def vmem(count):
    return [pl.BlockSpec(memory_space=pltpu.VMEM)] * count


def call(body, inputs, outputs, scratch=(), smem=0, name=None):
    return pl.pallas_call(
        body,
        out_shape=outputs,
        in_specs=[pl.BlockSpec(memory_space=pltpu.SMEM)] * smem + vmem(len(inputs) - smem),
        out_specs=vmem(len(outputs)) if isinstance(outputs, (tuple, list)) else vmem(1)[0],
        scratch_shapes=list(scratch),
        name=name,
    )(*inputs)


def faces_kernel(codes, p_ref, faces, send_a, send_b):
    tile_x, tile_y, slots, unknowns, edges = p_ref.shape
    _, even = place("gx")
    faces[...] = jnp.zeros_like(faces)
    for x in range(tile_x):
        for y in range(tile_y):
            for m in range(slots):
                faces[x, y, codes[x, y, m], 0:unknowns, :] = p_ref[x, y, m]
    send_a[...] = faces[jnp.where(even, tile_x - 1, 0), :, 0:5]
    send_b[...] = faces[jnp.where(even, 0, tile_x - 1), :, 0:5]


def x_sides(got_a, got_b, count_x):
    index, even = place("gx")

    def lower(y):
        value = jnp.where(even, got_b[y], got_a[y])
        return jnp.where(index > 0, value, jnp.zeros_like(value))

    def upper(y):
        value = jnp.where(even, got_a[y], got_b[y])
        return jnp.where(index < count_x - 1, value, jnp.zeros_like(value))

    return lower, upper


def strips_kernel(count_x):
    def body(faces, got_a, got_b, send_a, send_b):
        tile_x, tile_y = faces.shape[:2]
        _, even = place("gy")
        lower, upper = x_sides(got_a, got_b, count_x)
        for send, column in (
            (send_a, jnp.where(even, tile_y - 1, 0)),
            (send_b, jnp.where(even, 0, tile_y - 1)),
        ):
            send[0] = lower(column)
            send[tile_x + 1] = upper(column)
            for x in range(tile_x):
                send[1 + x] = faces[x, column, 0:5]

    return body


def terms_kernel(count_x, count_y, unknowns):
    span = 49 * unknowns
    lanes = -(-span // 128) * 128

    def body(
        a_codes, a_ref, faces, got_xa, got_xb, got_ya, got_yb,
        own, send_xa, send_xb, send_ya, send_yb,
        near, summed, coupled, total, side_x, side_y,
    ):
        tile_x, tile_y, slots, edges, _ = a_ref.shape
        _, even_x = place("gx")
        index_y, even_y = place("gy")
        wide = tile_y + 2
        lower, upper = x_sides(got_xa, got_xb, count_x)
        blank = (tile_x + 2) * wide
        flat = (5 * ROWS, edges)
        near[blank] = jnp.zeros(flat, near.dtype)
        for y in range(tile_y):
            near[1 + y] = lower(y).reshape(flat)
            near[(tile_x + 1) * wide + 1 + y] = upper(y).reshape(flat)
            for x in range(tile_x):
                near[(1 + x) * wide + 1 + y] = faces[x, y, 0:5].reshape(flat)
        for x in range(tile_x + 2):
            left = jnp.where(even_y, got_yb[x], got_ya[x])
            left = jnp.where(index_y > 0, left, jnp.zeros_like(left))
            near[x * wide] = left.reshape(flat)
            right = jnp.where(even_y, got_ya[x], got_yb[x])
            right = jnp.where(index_y < count_y - 1, right, jnp.zeros_like(right))
            near[x * wide + wide - 1] = right.reshape(flat)
        coupled[...] = jnp.zeros_like(coupled)
        total[...] = jnp.zeros_like(total)
        for x in range(tile_x):
            for y in range(tile_y):
                rows = summed.at[(x * tile_y + y) % summed.shape[0]]
                rows[...] = jnp.zeros(rows.shape, rows.dtype)
                for k in range(slots):
                    code = a_codes[x, y, k]
                    live = code < 9
                    step_x = lax.div(code, 3)
                    step_y = lax.rem(code, 3)
                    spot = jnp.where(live, (x + step_x) * wide + y + step_y, blank)
                    base = jnp.where(live, (step_x + 1) * 5 + step_y + 1, 12)
                    product = lax.dot_general(
                        near[spot], a_ref[x, y, k], NT, preferred_element_type=jnp.float32
                    )
                    for q, (face_x, face_y) in enumerate(face_steps):
                        rows[base + face_x * 5 + face_y] += product[q * ROWS : (q + 1) * ROWS]
                stack = coupled.at[(x * tile_y + y) % coupled.shape[0]]
                for o in range(25):
                    row = ((o // 5 + 1) * 7 + o % 5 + 1) * unknowns
                    stack[row : row + unknowns, :] = rows[o, 0:unknowns, :]
                terms = lax.dot_general(
                    near[(1 + x) * wide + 1 + y],
                    stack[...].astype(jnp.bfloat16),
                    NT,
                    preferred_element_type=jnp.float32,
                )
                for q, (face_x, face_y) in enumerate(face_steps):
                    part = terms[q * ROWS : (q + 1) * ROWS]
                    shift = (face_x * 7 + face_y) * unknowns
                    if shift:
                        part = pltpu.roll(part, (-shift) % lanes, 1)
                    to_x, to_y = x + face_x, y + face_y
                    if to_x < 0 or to_x >= tile_x:
                        side_x[0 if to_x < 0 else 1, y] = part
                    elif to_y < 0 or to_y >= tile_y:
                        side_y[0 if to_y < 0 else 1, x] = part
                    else:
                        total[to_x, to_y] += part
        own[...] = total[:, :, 0:unknowns, 0:span]
        for send, side, pick in (
            (send_xa, side_x, jnp.where(even_x, 1, 0)),
            (send_xb, side_x, jnp.where(even_x, 0, 1)),
            (send_ya, side_y, jnp.where(even_y, 1, 0)),
            (send_yb, side_y, jnp.where(even_y, 0, 1)),
        ):
            send[...] = side[pick].astype(send.dtype)

    return body


def sum_kernel(count_x, count_y):
    def body(own, got_xa, got_xb, got_ya, got_yb, result):
        tile_x, tile_y, unknowns, span = own.shape
        index_x, even_x = place("gx")
        index_y, even_y = place("gy")

        def shown(value, live):
            value = value[0:unknowns, 0:span].astype(jnp.float32)
            return jnp.where(live, value, jnp.zeros_like(value))

        result[...] = own[...]
        low_x, high_x = index_x > 0, index_x < count_x - 1
        low_y, high_y = index_y > 0, index_y < count_y - 1
        for y in range(tile_y):
            result[0, y] += shown(jnp.where(even_x, got_xb[y], got_xa[y]), low_x)
            result[tile_x - 1, y] += shown(jnp.where(even_x, got_xa[y], got_xb[y]), high_x)
        for x in range(tile_x):
            result[x, 0] += shown(jnp.where(even_y, got_yb[x], got_ya[x]), low_y)
            result[x, tile_y - 1] += shown(jnp.where(even_y, got_ya[x], got_yb[x]), high_y)

    return body


def solution(mesh):
    count_x, count_y = mesh.shape["gx"], mesh.shape["gy"]
    pairs = exchange_pairs(count_x, count_y)

    def shards(a_blocks, a_codes, p_blocks, p_codes):
        tile_x, tile_y, slots, edges, _ = a_blocks.shape
        unknowns = p_blocks.shape[3]
        span = 49 * unknowns
        lanes = -(-span // 128) * 128
        half = lambda *dims: jax.ShapeDtypeStruct(dims, jnp.bfloat16)
        block = (5, ROWS, edges)
        faces, send_a, send_b = call(
            faces_kernel,
            (p_codes, p_blocks),
            (half(tile_x, tile_y, 6, ROWS, edges), half(tile_y, *block), half(tile_y, *block)),
            smem=1,
            name="faces",
        )
        got_xa = lax.ppermute(send_a, AXES, pairs[0])
        got_xb = lax.ppermute(send_b, AXES, pairs[1])
        send_a, send_b = call(
            strips_kernel(count_x),
            (faces, got_xa, got_xb),
            (half(tile_x + 2, *block), half(tile_x + 2, *block)),
            name="strips",
        )
        got_ya = lax.ppermute(send_a, AXES, pairs[2])
        got_yb = lax.ppermute(send_b, AXES, pairs[3])
        own, *sends = call(
            terms_kernel(count_x, count_y, unknowns),
            (a_codes, a_blocks, faces, got_xa, got_xb, got_ya, got_yb),
            (
                jax.ShapeDtypeStruct((tile_x, tile_y, unknowns, span), jnp.float32),
                half(tile_y, ROWS, lanes),
                half(tile_y, ROWS, lanes),
                half(tile_x, ROWS, lanes),
                half(tile_x, ROWS, lanes),
            ),
            scratch=(
                pltpu.VMEM(((tile_x + 2) * (tile_y + 2) + 1, 5 * ROWS, edges), jnp.bfloat16),
                pltpu.VMEM((2, 25, ROWS, edges), jnp.float32),
                pltpu.VMEM((2, lanes, edges), jnp.float32),
                pltpu.VMEM((tile_x, tile_y, ROWS, lanes), jnp.float32),
                pltpu.VMEM((2, tile_y, ROWS, lanes), jnp.float32),
                pltpu.VMEM((2, tile_x, ROWS, lanes), jnp.float32),
            ),
            smem=1,
            name="terms",
        )
        got = [lax.ppermute(send, AXES, p) for send, p in zip(sends, pairs)]
        return call(
            sum_kernel(count_x, count_y),
            (own, *got),
            jax.ShapeDtypeStruct((tile_x, tile_y, unknowns, span), jnp.float32),
            name="sum",
        )

    in_specs = (
        P("gx", "gy", None, None, None),
        P("gx", "gy", None),
        P("gx", "gy", None, None, None),
        P("gx", "gy", None),
    )
    out_specs = P("gx", "gy", None, None)
    return jax.shard_map(shards, mesh=mesh, in_specs=in_specs, out_specs=out_specs, check_vma=False)
```

profile of v0, /device:TPU:4, one launch (start us, length us, event | category | flops | bytes accessed | tf_op | source)
XLA Modules:
  0.0 40.0 jit_solution(1055788704328201138)
XLA Ops:
  0.0 1.4 %copy.5.codes = s32[4,2,3]{2,1,0:T(2,128)} copy(s32[4,2,3]{0,1,2:T(2,128)} %param.7) | data formatting | bytes 192 | tf_op args[3]
  1.4 1.6 %copy.6.p_ref = bf16[4,2,3,12,192]{4,3,2,1,0:T(8,128)(2,1)} copy(bf16[4,2,3,12,192]{4,1,3,2,0:T(2,128)(2,1)} %param.6) | data formatting | bytes 221184 | tf_op args[2]
  3.0 1.8 %faces.1 = (bf16[4,2,6,16,192]{4,3,2,1,0:T(8,128)(2,1)}, bf16[2,5,16,192]{3,2,1,0:T(8,128)(2,1)}, bf16[2,5,16,192]{3,2,1,0:T(8,128)(2,1)}) custom-call(s32[4,2,3]{2,1,0:T(2,128)} %copy.5.codes, bf16[4,2,3,12,192]{4,3,2,1,0:T(8,128)(2,1)} %copy.6.p_ref), custom_call_target="tpu_custom_call" | custom-call | tf_op jit(solution)/shard_map/faces/pallas_call | solution.py:47
  4.8 1.5 %collective-permute-start = (bf16[2,5,16,192]{3,2,1,0:T(8,128)(2,1)}, bf16[2,5,16,192]{3,2,1,0:T(8,128)(2,1)S(1)}, u32[]{:S(2)}, u32[]{:S(2)}) collective-permute-start(bf16[2,5,16,192]{3,2,1,0:T(8,128)(2,1)} %get-tuple-element.16), channel_id=1, source_target_pairs={{0,8},{1,9},{2,10},{3,11},{4,12},{5,13},{6,14},{7,15},{8,0},{9,1},... | collective-permute-start | bytes 184328 | tf_op jit(solution)/shard_map/ppermute | solution.py:222
  6.3 0.0 collective-permute-start.1
  6.3 3.2 %collective-permute-done.got_a.got_xa = bf16[2,5,16,192]{3,2,1,0:T(8,128)(2,1)S(1)} collective-permute-done((bf16[2,5,16,192]{3,2,1,0:T(8,128)(2,1)}, bf16[2,5,16,192]{3,2,1,0:T(8,128)(2,1)S(1)}, u32[]{:S(2)}, u32[]{:S(2)}) %collective-permute-start) | collective-permute-done | bytes 61472 | tf_op jit(solution)/shard_map/ppermute | solution.py:222
  9.4 0.0 copy-start
  9.4 2.4 %collective-permute-done.1.got_b.got_xb = bf16[2,5,16,192]{3,2,1,0:T(8,128)(2,1)S(1)} collective-permute-done((bf16[2,5,16,192]{3,2,1,0:T(8,128)(2,1)}, bf16[2,5,16,192]{3,2,1,0:T(8,128)(2,1)S(1)}, u32[]{:S(2)}, u32[]{:S(2)}) %collective-permute-start.1) | collective-permute-done | bytes 61472 | tf_op jit(solution)/shard_map/ppermute | solution.py:223
  11.8 0.0 copy-start.1
  11.8 0.0 copy-done
  11.8 0.6 %copy-done.1 = bf16[2,5,16,192]{3,2,1,0:T(8,128)(2,1)} copy-done((bf16[2,5,16,192]{3,2,1,0:T(8,128)(2,1)}, bf16[2,5,16,192]{3,2,1,0:T(8,128)(2,1)S(1)}, u32[]{:S(2)}) %copy-start.1) | copy-done | bytes 61464
  12.4 1.8 %strips.1 = (bf16[6,5,16,192]{3,2,1,0:T(8,128)(2,1)}, bf16[6,5,16,192]{3,2,1,0:T(8,128)(2,1)}) custom-call(bf16[4,2,6,16,192]{4,3,2,1,0:T(8,128)(2,1)} %get-tuple-element.15.faces, bf16[2,5,16,192]{3,2,1,0:T(8,128)(2,1)} %copy-done, bf16[2,5,16,192]{3,2,1,0:T(8,128)(2,1)} %copy-done.1), custom_call_target="tpu_custom_call" | custom-call | tf_op jit(solution)/shard_map/strips/pallas_call | solution.py:47
  14.3 0.0 collective-permute-start.2
  14.3 0.0 collective-permute-start.3
  14.3 1.7 %collective-permute-done.2.got_ya = bf16[6,5,16,192]{3,2,1,0:T(8,128)(2,1)S(1)} collective-permute-done((bf16[6,5,16,192]{3,2,1,0:T(8,128)(2,1)}, bf16[6,5,16,192]{3,2,1,0:T(8,128)(2,1)S(1)}, u32[]{:S(2)}, u32[]{:S(2)}) %collective-permute-start.2) | collective-permute-done | bytes 184352 | tf_op jit(solution)/shard_map/ppermute | solution.py:230
  16.0 0.0 copy-start.2
  16.0 4.7 %collective-permute-done.3.got_yb = bf16[6,5,16,192]{3,2,1,0:T(8,128)(2,1)S(1)} collective-permute-done((bf16[6,5,16,192]{3,2,1,0:T(8,128)(2,1)}, bf16[6,5,16,192]{3,2,1,0:T(8,128)(2,1)S(1)}, u32[]{:S(2)}, u32[]{:S(2)}) %collective-permute-start.3) | collective-permute-done | bytes 184352 | tf_op jit(solution)/shard_map/ppermute | solution.py:231
  20.7 0.0 copy-done.2
  20.7 0.0 copy-start.3
  20.7 0.7 %copy-done.3 = bf16[6,5,16,192]{3,2,1,0:T(8,128)(2,1)} copy-done((bf16[6,5,16,192]{3,2,1,0:T(8,128)(2,1)}, bf16[6,5,16,192]{3,2,1,0:T(8,128)(2,1)S(1)}, u32[]{:S(2)}) %copy-start.3) | copy-done | bytes 184344
  21.4 7.0 %terms.1 = (f32[4,2,12,588]{3,2,1,0:T(8,128)}, bf16[2,16,640]{2,1,0:T(8,128)(2,1)}, bf16[2,16,640]{2,1,0:T(8,128)(2,1)}, bf16[4,16,640]{2,1,0:T(8,128)(2,1)}, bf16[4,16,640]{2,1,0:T(8,128)(2,1)}) custom-call(s32[4,2,5]{2,1,0:T(2,128)} %a_codes.1, bf16[4,2,5,192,192]{4,3,2,1,0:T(8,128)(2,1)} %a_ref.1, bf16[4,2,6,16,192]{4,3,2,1,0:T(8,128)(2,1)} %get-tuple-element.15.faces, ...), custom_call_target="tpu_custom_call" | custom-call | tf_op jit(solution)/shard_map/terms/pallas_call | solution.py:47
  28.4 0.1 collective-permute-start.6
  28.5 0.0 collective-permute-start.7
  28.5 2.0 %collective-permute-start.4 = (bf16[2,16,640]{2,1,0:T(8,128)(2,1)}, bf16[2,16,640]{2,1,0:T(8,128)(2,1)S(1)}, u32[]{:S(2)}, u32[]{:S(2)}) collective-permute-start(bf16[2,16,640]{2,1,0:T(8,128)(2,1)} %get-tuple-element.21), channel_id=1, source_target_pairs={{0,8},{1,9},{2,10},{3,11},{4,12},{5,13},{6,14},{7,15},{8,0},{9,1},... | collective-permute-start | bytes 122888 | tf_op jit(solution)/shard_map/ppermute | solution.py:253
  30.5 1.5 %collective-permute-start.5 = (bf16[2,16,640]{2,1,0:T(8,128)(2,1)}, bf16[2,16,640]{2,1,0:T(8,128)(2,1)S(1)}, u32[]{:S(2)}, u32[]{:S(2)}) collective-permute-start(bf16[2,16,640]{2,1,0:T(8,128)(2,1)} %get-tuple-element.22), channel_id=1, source_target_pairs={{0,1},{1,0},{2,3},{3,2},{4,5},{5,4},{6,7},{7,6},{8,16},{9,17},{10,... | collective-permute-start | bytes 122888 | tf_op jit(solution)/shard_map/ppermute | solution.py:253
  32.0 2.0 %collective-permute-done.4.got_xa = bf16[2,16,640]{2,1,0:T(8,128)(2,1)S(1)} collective-permute-done((bf16[2,16,640]{2,1,0:T(8,128)(2,1)}, bf16[2,16,640]{2,1,0:T(8,128)(2,1)S(1)}, u32[]{:S(2)}, u32[]{:S(2)}) %collective-permute-start.4) | collective-permute-done | bytes 40992 | tf_op jit(solution)/shard_map/ppermute | solution.py:253
  34.0 0.0 copy-start.6
  34.0 1.6 %collective-permute-done.5.got_xb = bf16[2,16,640]{2,1,0:T(8,128)(2,1)S(1)} collective-permute-done((bf16[2,16,640]{2,1,0:T(8,128)(2,1)}, bf16[2,16,640]{2,1,0:T(8,128)(2,1)S(1)}, u32[]{:S(2)}, u32[]{:S(2)}) %collective-permute-start.5) | collective-permute-done | bytes 40992 | tf_op jit(solution)/shard_map/ppermute | solution.py:253
  35.6 0.0 copy-start.7
  35.6 0.0 collective-permute-done.6.got_ya
  35.6 0.0 copy-start.4
  35.6 0.0 collective-permute-done.7.got_yb
  35.7 0.0 copy-start.5
  35.7 0.0 copy-done.6
  35.7 0.6 %copy-done.7 = bf16[2,16,640]{2,1,0:T(8,128)(2,1)} copy-done((bf16[2,16,640]{2,1,0:T(8,128)(2,1)}, bf16[2,16,640]{2,1,0:T(8,128)(2,1)S(1)}, u32[]{:S(2)}) %copy-start.7) | copy-done | bytes 40984
  36.2 0.0 copy-done.4
  36.3 0.0 copy-done.5
  36.3 1.9 %sum.1 = f32[4,2,12,588]{3,2,1,0:T(8,128)} custom-call(f32[4,2,12,588]{3,2,1,0:T(8,128)} %get-tuple-element.20.own, bf16[2,16,640]{2,1,0:T(8,128)(2,1)} %copy-done.6, bf16[2,16,640]{2,1,0:T(8,128)(2,1)} %copy-done.7, bf16[4,16,640]{2,1,0:T(8,128)(2,1)} %copy-done.4, bf16[4,16,640]{2,1,0:T(8,128)(2,1)} %copy-done.5), custom_call_target="tpu_custom_call" | custom-call | tf_op jit(solution)/shard_map/sum/pallas_call | solution.py:47
  38.2 1.8 %copy.7 = f32[4,2,12,588]{3,1,2,0:T(2,128)} copy(f32[4,2,12,588]{3,2,1,0:T(8,128)} %sum.1) | data formatting | bytes 451584 | tf_op jit(solution)/shard_map/sum/pallas_call | solution.py:47
Async XLA Ops:
  4.8 4.7 %collective-permute-start = (bf16[2,5,16,192]{3,2,1,0:T(8,128)(2,1)}, bf16[2,5,16,192]{3,2,1,0:T(8,128)(2,1)S(1)}, u32[]{:S(2)}, u32[]{:S(2)}) collective-permute-start(bf16[2,5,16,192]{3,2,1,0:T(8,128)(2,1)} %get-tuple-element.16), channel_id=1, source_target_pairs={{0,8},{1,9},{2,10},{3,11},{4,12},{5,13},{6,14},{7,15},{8,0},{9,1},... | collective-permute-start | bytes 184328 | tf_op jit(solution)/shard_map/ppermute | solution.py:222
  6.3 5.6 %collective-permute-start.1 = (bf16[2,5,16,192]{3,2,1,0:T(8,128)(2,1)}, bf16[2,5,16,192]{3,2,1,0:T(8,128)(2,1)S(1)}, u32[]{:S(2)}, u32[]{:S(2)}) collective-permute-start(bf16[2,5,16,192]{3,2,1,0:T(8,128)(2,1)} %get-tuple-element.17), channel_id=1, source_target_pairs={{0,1},{1,0},{2,3},{3,2},{4,5},{5,4},{6,7},{7,6},{8,16},{9,17},{10,... | collective-permute-start | bytes 184328 | tf_op jit(solution)/shard_map/ppermute | solution.py:223
  9.4 2.4 %copy-start = (bf16[2,5,16,192]{3,2,1,0:T(8,128)(2,1)}, bf16[2,5,16,192]{3,2,1,0:T(8,128)(2,1)S(1)}, u32[]{:S(2)}) copy-start(bf16[2,5,16,192]{3,2,1,0:T(8,128)(2,1)S(1)} %collective-permute-done.got_a.got_xa) | copy-start | bytes 184324
  11.8 0.6 %copy-start.1 = (bf16[2,5,16,192]{3,2,1,0:T(8,128)(2,1)}, bf16[2,5,16,192]{3,2,1,0:T(8,128)(2,1)S(1)}, u32[]{:S(2)}) copy-start(bf16[2,5,16,192]{3,2,1,0:T(8,128)(2,1)S(1)} %collective-permute-done.1.got_b.got_xb) | copy-start | bytes 184324
  14.3 1.7 %collective-permute-start.2 = (bf16[6,5,16,192]{3,2,1,0:T(8,128)(2,1)}, bf16[6,5,16,192]{3,2,1,0:T(8,128)(2,1)S(1)}, u32[]{:S(2)}, u32[]{:S(2)}) collective-permute-start(bf16[6,5,16,192]{3,2,1,0:T(8,128)(2,1)} %get-tuple-element.18), channel_id=1, source_target_pairs={{0,1},{8,9},{16,17},{24,25},{1,0},{9,8},{17,16},{25,24},{2,3},{10,... | collective-permute-start | bytes 552968 | tf_op jit(solution)/shard_map/ppermute | solution.py:230
  14.3 6.4 %collective-permute-start.3 = (bf16[6,5,16,192]{3,2,1,0:T(8,128)(2,1)}, bf16[6,5,16,192]{3,2,1,0:T(8,128)(2,1)S(1)}, u32[]{:S(2)}, u32[]{:S(2)}) collective-permute-start(bf16[6,5,16,192]{3,2,1,0:T(8,128)(2,1)} %get-tuple-element.19), channel_id=1, source_target_pairs={{0,8},{8,0},{16,24},{24,16},{1,2},{9,10},{17,18},{25,26},{2,1},{10... | collective-permute-start | bytes 552968 | tf_op jit(solution)/shard_map/ppermute | solution.py:231
  16.0 4.7 %copy-start.2 = (bf16[6,5,16,192]{3,2,1,0:T(8,128)(2,1)}, bf16[6,5,16,192]{3,2,1,0:T(8,128)(2,1)S(1)}, u32[]{:S(2)}) copy-start(bf16[6,5,16,192]{3,2,1,0:T(8,128)(2,1)S(1)} %collective-permute-done.2.got_ya) | copy-start | bytes 552964
  20.7 0.7 %copy-start.3 = (bf16[6,5,16,192]{3,2,1,0:T(8,128)(2,1)}, bf16[6,5,16,192]{3,2,1,0:T(8,128)(2,1)S(1)}, u32[]{:S(2)}) copy-start(bf16[6,5,16,192]{3,2,1,0:T(8,128)(2,1)S(1)} %collective-permute-done.3.got_yb) | copy-start | bytes 552964
  28.4 7.3 %collective-permute-start.6 = (bf16[4,16,640]{2,1,0:T(8,128)(2,1)}, bf16[4,16,640]{2,1,0:T(8,128)(2,1)S(1)}, u32[]{:S(2)}, u32[]{:S(2)}) collective-permute-start(bf16[4,16,640]{2,1,0:T(8,128)(2,1)} %get-tuple-element.23), channel_id=1, source_target_pairs={{0,1},{8,9},{16,17},{24,25},{1,0},{9,8},{17,16},{25,24},{2,3},{10,... | collective-permute-start | bytes 245768 | tf_op jit(solution)/shard_map/ppermute | solution.py:253
  28.5 7.1 %collective-permute-start.7 = (bf16[4,16,640]{2,1,0:T(8,128)(2,1)}, bf16[4,16,640]{2,1,0:T(8,128)(2,1)S(1)}, u32[]{:S(2)}, u32[]{:S(2)}) collective-permute-start(bf16[4,16,640]{2,1,0:T(8,128)(2,1)} %get-tuple-element.24), channel_id=1, source_target_pairs={{0,8},{8,0},{16,24},{24,16},{1,2},{9,10},{17,18},{25,26},{2,1},{10... | collective-permute-start | bytes 245768 | tf_op jit(solution)/shard_map/ppermute | solution.py:253
  28.5 5.5 %collective-permute-start.4 = (bf16[2,16,640]{2,1,0:T(8,128)(2,1)}, bf16[2,16,640]{2,1,0:T(8,128)(2,1)S(1)}, u32[]{:S(2)}, u32[]{:S(2)}) collective-permute-start(bf16[2,16,640]{2,1,0:T(8,128)(2,1)} %get-tuple-element.21), channel_id=1, source_target_pairs={{0,8},{1,9},{2,10},{3,11},{4,12},{5,13},{6,14},{7,15},{8,0},{9,1},... | collective-permute-start | bytes 122888 | tf_op jit(solution)/shard_map/ppermute | solution.py:253
  30.5 5.1 %collective-permute-start.5 = (bf16[2,16,640]{2,1,0:T(8,128)(2,1)}, bf16[2,16,640]{2,1,0:T(8,128)(2,1)S(1)}, u32[]{:S(2)}, u32[]{:S(2)}) collective-permute-start(bf16[2,16,640]{2,1,0:T(8,128)(2,1)} %get-tuple-element.22), channel_id=1, source_target_pairs={{0,1},{1,0},{2,3},{3,2},{4,5},{5,4},{6,7},{7,6},{8,16},{9,17},{10,... | collective-permute-start | bytes 122888 | tf_op jit(solution)/shard_map/ppermute | solution.py:253
  34.0 1.6 %copy-start.6 = (bf16[2,16,640]{2,1,0:T(8,128)(2,1)}, bf16[2,16,640]{2,1,0:T(8,128)(2,1)S(1)}, u32[]{:S(2)}) copy-start(bf16[2,16,640]{2,1,0:T(8,128)(2,1)S(1)} %collective-permute-done.4.got_xa) | copy-start | bytes 122884
  35.6 0.6 %copy-start.7 = (bf16[2,16,640]{2,1,0:T(8,128)(2,1)}, bf16[2,16,640]{2,1,0:T(8,128)(2,1)S(1)}, u32[]{:S(2)}) copy-start(bf16[2,16,640]{2,1,0:T(8,128)(2,1)S(1)} %collective-permute-done.5.got_xb) | copy-start | bytes 122884
  35.6 0.6 %copy-start.4 = (bf16[4,16,640]{2,1,0:T(8,128)(2,1)}, bf16[4,16,640]{2,1,0:T(8,128)(2,1)S(1)}, u32[]{:S(2)}) copy-start(bf16[4,16,640]{2,1,0:T(8,128)(2,1)S(1)} %collective-permute-done.6.got_ya) | copy-start | bytes 245764
  35.7 0.7 %copy-start.5 = (bf16[4,16,640]{2,1,0:T(8,128)(2,1)}, bf16[4,16,640]{2,1,0:T(8,128)(2,1)S(1)}, u32[]{:S(2)}) copy-start(bf16[4,16,640]{2,1,0:T(8,128)(2,1)S(1)} %collective-permute-done.7.got_yb) | copy-start | bytes 245764
where the time goes:
time: 40.7 us; the launch traced here: 40 us
  waiting for transfers between devices  15.6 us (38%)
  Pallas kernels  12.5 us (31%)
  local copies, waits for them, and re-layouts  6.74 us (17%)
  starting transfers between devices  5.13 us (13%)
    pallas_call x4, Pallas kernels, call(): pl.pallas_call(body, out_shape=outputs, in_specs=[pl.BlockSpec(memory_spa...  12.5 us
    unnamed x18, local copies, waits for them, and re-layouts  4.95 us
    ppermute x1, waiting for transfers between devices, shards(): got_yb = lax.ppermute(send_b, AXES, pairs[3])  4.69 us
    ppermute x4, starting transfers between devices, shards(): got = [lax.ppermute(send, AXES, p) for send, p in zip(sends, pairs)]  3.63 us
    ppermute x4, waiting for transfers between devices, shards(): got = [lax.ppermute(send, AXES, p) for send, p in zip(sends, pairs)]  3.62 us
    ppermute x1, waiting for transfers between devices, shards(): got_xa = lax.ppermute(send_a, AXES, pairs[0])  3.16 us
    ppermute x1, waiting for transfers between devices, shards(): got_xb = lax.ppermute(send_b, AXES, pairs[1])  2.39 us
    pallas_call x1, local copies, waits for them, and re-layouts, call(): pl.pallas_call(body, out_shape=outputs, in_specs=[pl.BlockSpec(memory_spa...  1.79 us
  transfers between devices with their start and end apart: 8, of which 6 were waited for; matrix products, arithmetic and copies ran while one was open for 0% of the time, Pallas kernels for 0%

commit v1 on v0

--- a/solution.py
+++ b/solution.py
@@ -50,18 +50,20 @@
         in_specs=[pl.BlockSpec(memory_space=pltpu.SMEM)] * smem + vmem(len(inputs) - smem),
         out_specs=vmem(len(outputs)) if isinstance(outputs, (tuple, list)) else vmem(1)[0],
         scratch_shapes=list(scratch),
+        compiler_params=pltpu.CompilerParams(vmem_limit_bytes=20 << 20),
         name=name,
     )(*inputs)
 
 
 def faces_kernel(codes, p_ref, faces, send_a, send_b):
-    tile_x, tile_y, slots, unknowns, edges = p_ref.shape
+    tile_x, slots, unknowns, tile_y, edges = p_ref.shape
     _, even = place("gx")
     faces[...] = jnp.zeros_like(faces)
     for x in range(tile_x):
-        for y in range(tile_y):
-            for m in range(slots):
-                faces[x, y, codes[x, y, m], 0:unknowns, :] = p_ref[x, y, m]
+        for m in range(slots):
+            rows = p_ref[x, m]
+            for y in range(tile_y):
+                faces[x, y, codes[m, y, x], 0:unknowns, :] = rows[:, y, :]
     send_a[...] = faces[jnp.where(even, tile_x - 1, 0), :, 0:5]
     send_b[...] = faces[jnp.where(even, 0, tile_x - 1), :, 0:5]
 
@@ -188,15 +190,20 @@
             value = value[0:unknowns, 0:span].astype(jnp.float32)
             return jnp.where(live, value, jnp.zeros_like(value))
 
-        result[...] = own[...]
         low_x, high_x = index_x > 0, index_x < count_x - 1
         low_y, high_y = index_y > 0, index_y < count_y - 1
-        for y in range(tile_y):
-            result[0, y] += shown(jnp.where(even_x, got_xb[y], got_xa[y]), low_x)
-            result[tile_x - 1, y] += shown(jnp.where(even_x, got_xa[y], got_xb[y]), high_x)
         for x in range(tile_x):
-            result[x, 0] += shown(jnp.where(even_y, got_yb[x], got_ya[x]), low_y)
-            result[x, tile_y - 1] += shown(jnp.where(even_y, got_ya[x], got_yb[x]), high_y)
+            for y in range(tile_y):
+                value = own[x, y]
+                if x == 0:
+                    value += shown(jnp.where(even_x, got_xb[y], got_xa[y]), low_x)
+                if x == tile_x - 1:
+                    value += shown(jnp.where(even_x, got_xa[y], got_xb[y]), high_x)
+                if y == 0:
+                    value += shown(jnp.where(even_y, got_yb[x], got_ya[x]), low_y)
+                if y == tile_y - 1:
+                    value += shown(jnp.where(even_y, got_ya[x], got_yb[x]), high_y)
+                result[x, :, y, :] = value
 
     return body
 
@@ -214,7 +221,7 @@
         block = (5, ROWS, edges)
         faces, send_a, send_b = call(
             faces_kernel,
-            (p_codes, p_blocks),
+            (jnp.transpose(p_codes, (2, 1, 0)), jnp.transpose(p_blocks, (0, 2, 3, 1, 4))),
             (half(tile_x, tile_y, 6, ROWS, edges), half(tile_y, *block), half(tile_y, *block)),
             smem=1,
             name="faces",
@@ -251,12 +258,13 @@
             name="terms",
         )
         got = [lax.ppermute(send, AXES, p) for send, p in zip(sends, pairs)]
-        return call(
+        result = call(
             sum_kernel(count_x, count_y),
             (own, *got),
-            jax.ShapeDtypeStruct((tile_x, tile_y, unknowns, span), jnp.float32),
+            jax.ShapeDtypeStruct((tile_x, unknowns, tile_y, span), jnp.float32),
             name="sum",
         )
+        return jnp.transpose(result, (0, 2, 1, 3))
 
     in_specs = (
         P("gx", "gy", None, None, None),

time: 40.7 us -> 31.5 us (0.77)
  the two profiles are of different devices: /device:TPU:4 before, /device:TPU:0 now
where the time goes in v1:
time: 31.5 us; the launch traced here: 31.3 us
  starting transfers between devices  11 us (35%)
  waiting for transfers between devices  9.78 us (31%)
  Pallas kernels  6.11 us (19%)
  local copies, waits for them, and re-layouts  4.39 us (14%)
    pallas_call x4, Pallas kernels, call(): pl.pallas_call(body, out_shape=outputs, in_specs=[pl.BlockSpec(memory_spa...  6.11 us
    ppermute x1, starting transfers between devices, shards(): got_yb = lax.ppermute(send_b, AXES, pairs[3])  4.51 us
    unnamed x8, local copies, waits for them, and re-layouts  4.39 us
    ppermute x1, waiting for transfers between devices, shards(): got_yb = lax.ppermute(send_b, AXES, pairs[3])  4.17 us
    ppermute x4, starting transfers between devices, shards(): got = [lax.ppermute(send, AXES, p) for send, p in zip(sends, pairs)]  3.35 us
    ppermute x4, waiting for transfers between devices, shards(): got = [lax.ppermute(send, AXES, p) for send, p in zip(sends, pairs)]  3.16 us
    ppermute x1, starting transfers between devices, shards(): got_xa = lax.ppermute(send_a, AXES, pairs[0])  3.03 us
    ppermute x1, waiting for transfers between devices, shards(): got_xa = lax.ppermute(send_a, AXES, pairs[0])  2.44 us
  transfers between devices with their start and end apart: 8, of which 3 were waited for; matrix products, arithmetic and copies ran while one was open for 0% of the time, Pallas kernels for 0%

profile of v1, /device:TPU:0, one launch (start us, length us, event | category | flops | bytes accessed | tf_op | source)
XLA Modules:
  0.0 31.3 jit_solution(5992739952013642557)
XLA Ops:
  0.0 0.0 copy-start.1
  0.0 0.9 %copy-done.1 = bf16[4,2,3,12,192]{4,1,3,2,0:T(2,128)(2,1)S(1)} copy-done((bf16[4,2,3,12,192]{4,1,3,2,0:T(2,128)(2,1)S(1)}, bf16[4,2,3,12,192]{4,1,3,2,0:T(2,128)(2,1)}, u32[]{:S(2)}) %copy-start.1) | copy-done | bytes 110616
  0.9 0.0 copy-start.3
  0.9 0.7 %copy-done.3 = s32[4,2,3]{0,1,2:T(2,128)S(1)} copy-done((s32[4,2,3]{0,1,2:T(2,128)S(1)}, s32[4,2,3]{0,1,2:T(2,128)}, u32[]{:S(2)}) %copy-start.3) | copy-done | bytes 120
  1.6 0.9 %faces.1 = (bf16[4,2,6,16,192]{4,3,2,1,0:T(8,128)(2,1)S(1)}, bf16[2,5,16,192]{3,2,1,0:T(8,128)(2,1)S(1)}, bf16[2,5,16,192]{3,2,1,0:T(8,128)(2,1)S(1)}) custom-call(s32[3,2,4]{2,1,0:T(2,128)S(1)} %bitcast.4, bf16[4,3,12,2,192]{4,3,2,1,0:T(2,128)(2,1)S(1)} %bitcast.3), custom_call_target="tpu_custom_call" | custom-call | tf_op jit(solution)/shard_map/faces/pallas_call | solution.py:47
  2.5 3.0 %collective-permute-start = (bf16[2,5,16,192]{3,2,1,0:T(8,128)(2,1)S(1)}, bf16[2,5,16,192]{3,2,1,0:T(8,128)(2,1)S(1)}, u32[]{:S(2)}, u32[]{:S(2)}) collective-permute-start(bf16[2,5,16,192]{3,2,1,0:T(8,128)(2,1)S(1)} %get-tuple-element.16), channel_id=1, source_target_pairs={{0,8},{1,9},{2,10},{3,11},{4,12},{5,13},{6,14},{7,15},{8,0},{9,1},... | collective-permute-start | bytes 184328 | tf_op jit(solution)/shard_map/ppermute | solution.py:229
  5.5 0.0 collective-permute-start.1
  5.5 2.4 %collective-permute-done.got_a.got_xa = bf16[2,5,16,192]{3,2,1,0:T(8,128)(2,1)S(1)} collective-permute-done((bf16[2,5,16,192]{3,2,1,0:T(8,128)(2,1)S(1)}, bf16[2,5,16,192]{3,2,1,0:T(8,128)(2,1)S(1)}, u32[]{:S(2)}, u32[]{:S(2)}) %collective-permute-start) | collective-permute-done | bytes 61472 | tf_op jit(solution)/shard_map/ppermute | solution.py:229
  7.9 0.0 collective-permute-done.1.got_b.got_xb
  8.0 0.1 collective-permute-start.2
  8.1 4.5 %collective-permute-start.3 = (bf16[6,5,16,192]{3,2,1,0:T(8,128)(2,1)S(1)}, bf16[6,5,16,192]{3,2,1,0:T(8,128)(2,1)S(1)}, u32[]{:S(2)}, u32[]{:S(2)}) collective-permute-start(bf16[6,5,16,192]{3,2,1,0:T(8,128)(2,1)S(1)} %get-tuple-element.19), channel_id=1, source_target_pairs={{0,8},{8,0},{16,24},{24,16},{1,2},{9,10},{17,18},{25,26},{2,1},{10... | collective-permute-start | bytes 552968 | tf_op jit(solution)/shard_map/ppermute | solution.py:238
  12.6 0.0 collective-permute-done.2.got_ya
  12.6 4.2 %collective-permute-done.3.got_yb = bf16[6,5,16,192]{3,2,1,0:T(8,128)(2,1)S(1)} collective-permute-done((bf16[6,5,16,192]{3,2,1,0:T(8,128)(2,1)S(1)}, bf16[6,5,16,192]{3,2,1,0:T(8,128)(2,1)S(1)}, u32[]{:S(2)}, u32[]{:S(2)}) %collective-permute-start.3) | collective-permute-done | bytes 184352 | tf_op jit(solution)/shard_map/ppermute | solution.py:238
  16.8 0.0 copy-start
  16.8 2.1 %copy-done = bf16[4,2,5,192,192]{4,3,2,1,0:T(8,128)(2,1)S(1)} copy-done((bf16[4,2,5,192,192]{4,3,2,1,0:T(8,128)(2,1)S(1)}, bf16[4,2,5,192,192]{4,3,2,1,0:T(8,128)(2,1)}, u32[]{:S(2)}) %copy-start) | copy-done | bytes 2949144
  18.9 0.0 copy-start.2
  18.9 0.7 %copy-done.2 = s32[4,2,5]{2,1,0:T(2,128)S(1)} copy-done((s32[4,2,5]{2,1,0:T(2,128)S(1)}, s32[4,2,5]{2,1,0:T(2,128)}, u32[]{:S(2)}) %copy-start.2) | copy-done | bytes 184
  19.6 4.4 %terms.1 = (f32[4,2,12,588]{3,2,1,0:T(8,128)S(1)}, bf16[2,16,640]{2,1,0:T(8,128)(2,1)S(1)}, bf16[2,16,640]{2,1,0:T(8,128)(2,1)S(1)}, bf16[4,16,640]{2,1,0:T(8,128)(2,1)S(1)}, bf16[4,16,640]{2,1,0:T(8,128)(2,1)S(1)}) custom-call(s32[4,2,5]{2,1,0:T(2,128)S(1)} %copy-done.2, bf16[4,2,5,192,192]{4,3,2,1,0:T(8,128)(2,1)S(1)} %copy-done, ...), custom_call_target="tpu_custom_call" | custom-call | tf_op jit(solution)/shard_map/terms/pallas_call | solution.py:47
  23.9 0.1 collective-permute-start.6
  24.0 2.1 %collective-permute-start.7 = (bf16[4,16,640]{2,1,0:T(8,128)(2,1)S(1)}, bf16[4,16,640]{2,1,0:T(8,128)(2,1)S(1)}, u32[]{:S(2)}, u32[]{:S(2)}) collective-permute-start(bf16[4,16,640]{2,1,0:T(8,128)(2,1)S(1)} %get-tuple-element.24), channel_id=1, source_target_pairs={{0,8},{8,0},{16,24},{24,16},{1,2},{9,10},{17,18},{25,26},{2,1},{10... | collective-permute-start | bytes 245768 | tf_op jit(solution)/shard_map/ppermute | solution.py:260
  26.1 0.0 collective-permute-start.4
  26.2 1.1 %collective-permute-start.5 = (bf16[2,16,640]{2,1,0:T(8,128)(2,1)S(1)}, bf16[2,16,640]{2,1,0:T(8,128)(2,1)S(1)}, u32[]{:S(2)}, u32[]{:S(2)}) collective-permute-start(bf16[2,16,640]{2,1,0:T(8,128)(2,1)S(1)} %get-tuple-element.22), channel_id=1, source_target_pairs={{0,1},{1,0},{2,3},{3,2},{4,5},{5,4},{6,7},{7,6},{8,16},{9,17},{10,... | collective-permute-start | bytes 122888 | tf_op jit(solution)/shard_map/ppermute | solution.py:260
  27.3 3.1 %collective-permute-done.4.got_xa = bf16[2,16,640]{2,1,0:T(8,128)(2,1)S(1)} collective-permute-done((bf16[2,16,640]{2,1,0:T(8,128)(2,1)S(1)}, bf16[2,16,640]{2,1,0:T(8,128)(2,1)S(1)}, u32[]{:S(2)}, u32[]{:S(2)}) %collective-permute-start.4) | collective-permute-done | bytes 40992 | tf_op jit(solution)/shard_map/ppermute | solution.py:260
  30.4 0.0 collective-permute-done.5.got_xb
  30.4 0.0 collective-permute-done.6.got_ya
  30.5 0.0 collective-permute-done.7.got_yb
  30.5 0.8 %sum.1 = f32[4,12,2,588]{3,2,1,0:T(2,128)} custom-call(f32[4,2,12,588]{3,2,1,0:T(8,128)S(1)} %get-tuple-element.20.own, bf16[2,16,640]{2,1,0:T(8,128)(2,1)S(1)} %collective-permute-done.4.got_xa, bf16[2,16,640]{2,1,0:T(8,128)(2,1)S(1)} %collective-permute-done.5.got_xb, bf16[4,16,640]{2,1,0:T(8,128)(2,1)S(1)} %collective-permute-done.6.got_ya, ...), custom_call_target="tpu_custom_call" | custom-call | tf_op jit(solution)/shard_map/sum/pallas_call | solution.py:47
  (1 shorter events, 0.0 us)
Async XLA Ops:
  0.0 0.9 %copy-start.1 = (bf16[4,2,3,12,192]{4,1,3,2,0:T(2,128)(2,1)S(1)}, bf16[4,2,3,12,192]{4,1,3,2,0:T(2,128)(2,1)}, u32[]{:S(2)}) copy-start(bf16[4,2,3,12,192]{4,1,3,2,0:T(2,128)(2,1)} %param.6) | copy-start | bytes 331780
  0.9 0.7 %copy-start.3 = (s32[4,2,3]{0,1,2:T(2,128)S(1)}, s32[4,2,3]{0,1,2:T(2,128)}, u32[]{:S(2)}) copy-start(s32[4,2,3]{0,1,2:T(2,128)} %param.7) | copy-start | bytes 292
  2.5 5.5 %collective-permute-start = (bf16[2,5,16,192]{3,2,1,0:T(8,128)(2,1)S(1)}, bf16[2,5,16,192]{3,2,1,0:T(8,128)(2,1)S(1)}, u32[]{:S(2)}, u32[]{:S(2)}) collective-permute-start(bf16[2,5,16,192]{3,2,1,0:T(8,128)(2,1)S(1)} %get-tuple-element.16), channel_id=1, source_target_pairs={{0,8},{1,9},{2,10},{3,11},{4,12},{5,13},{6,14},{7,15},{8,0},{9,1},... | collective-permute-start | bytes 184328 | tf_op jit(solution)/shard_map/ppermute | solution.py:229
  5.5 2.4 %collective-permute-start.1 = (bf16[2,5,16,192]{3,2,1,0:T(8,128)(2,1)S(1)}, bf16[2,5,16,192]{3,2,1,0:T(8,128)(2,1)S(1)}, u32[]{:S(2)}, u32[]{:S(2)}) collective-permute-start(bf16[2,5,16,192]{3,2,1,0:T(8,128)(2,1)S(1)} %get-tuple-element.17), channel_id=1, source_target_pairs={{0,1},{1,0},{2,3},{3,2},{4,5},{5,4},{6,7},{7,6},{8,16},{9,17},{10,... | collective-permute-start | bytes 184328 | tf_op jit(solution)/shard_map/ppermute | solution.py:230
  8.0 4.6 %collective-permute-start.2 = (bf16[6,5,16,192]{3,2,1,0:T(8,128)(2,1)S(1)}, bf16[6,5,16,192]{3,2,1,0:T(8,128)(2,1)S(1)}, u32[]{:S(2)}, u32[]{:S(2)}) collective-permute-start(bf16[6,5,16,192]{3,2,1,0:T(8,128)(2,1)S(1)} %get-tuple-element.18), channel_id=1, source_target_pairs={{0,1},{8,9},{16,17},{24,25},{1,0},{9,8},{17,16},{25,24},{2,3},{10,... | collective-permute-start | bytes 552968 | tf_op jit(solution)/shard_map/ppermute | solution.py:237
  8.1 8.7 %collective-permute-start.3 = (bf16[6,5,16,192]{3,2,1,0:T(8,128)(2,1)S(1)}, bf16[6,5,16,192]{3,2,1,0:T(8,128)(2,1)S(1)}, u32[]{:S(2)}, u32[]{:S(2)}) collective-permute-start(bf16[6,5,16,192]{3,2,1,0:T(8,128)(2,1)S(1)} %get-tuple-element.19), channel_id=1, source_target_pairs={{0,8},{8,0},{16,24},{24,16},{1,2},{9,10},{17,18},{25,26},{2,1},{10... | collective-permute-start | bytes 552968 | tf_op jit(solution)/shard_map/ppermute | solution.py:238
  16.8 2.1 %copy-start = (bf16[4,2,5,192,192]{4,3,2,1,0:T(8,128)(2,1)S(1)}, bf16[4,2,5,192,192]{4,3,2,1,0:T(8,128)(2,1)}, u32[]{:S(2)}) copy-start(bf16[4,2,5,192,192]{4,3,2,1,0:T(8,128)(2,1)} %a_ref.1) | copy-start | bytes 8847364
  18.9 0.7 %copy-start.2 = (s32[4,2,5]{2,1,0:T(2,128)S(1)}, s32[4,2,5]{2,1,0:T(2,128)}, u32[]{:S(2)}) copy-start(s32[4,2,5]{2,1,0:T(2,128)} %a_codes.1) | copy-start | bytes 484
  23.9 6.5 %collective-permute-start.6 = (bf16[4,16,640]{2,1,0:T(8,128)(2,1)S(1)}, bf16[4,16,640]{2,1,0:T(8,128)(2,1)S(1)}, u32[]{:S(2)}, u32[]{:S(2)}) collective-permute-start(bf16[4,16,640]{2,1,0:T(8,128)(2,1)S(1)} %get-tuple-element.23), channel_id=1, source_target_pairs={{0,1},{8,9},{16,17},{24,25},{1,0},{9,8},{17,16},{25,24},{2,3},{10,... | collective-permute-start | bytes 245768 | tf_op jit(solution)/shard_map/ppermute | solution.py:260
  24.0 6.4 %collective-permute-start.7 = (bf16[4,16,640]{2,1,0:T(8,128)(2,1)S(1)}, bf16[4,16,640]{2,1,0:T(8,128)(2,1)S(1)}, u32[]{:S(2)}, u32[]{:S(2)}) collective-permute-start(bf16[4,16,640]{2,1,0:T(8,128)(2,1)S(1)} %get-tuple-element.24), channel_id=1, source_target_pairs={{0,8},{8,0},{16,24},{24,16},{1,2},{9,10},{17,18},{25,26},{2,1},{10... | collective-permute-start | bytes 245768 | tf_op jit(solution)/shard_map/ppermute | solution.py:260
  26.1 4.3 %collective-permute-start.4 = (bf16[2,16,640]{2,1,0:T(8,128)(2,1)S(1)}, bf16[2,16,640]{2,1,0:T(8,128)(2,1)S(1)}, u32[]{:S(2)}, u32[]{:S(2)}) collective-permute-start(bf16[2,16,640]{2,1,0:T(8,128)(2,1)S(1)} %get-tuple-element.21), channel_id=1, source_target_pairs={{0,8},{1,9},{2,10},{3,11},{4,12},{5,13},{6,14},{7,15},{8,0},{9,1},... | collective-permute-start | bytes 122888 | tf_op jit(solution)/shard_map/ppermute | solution.py:260
  26.2 4.3 %collective-permute-start.5 = (bf16[2,16,640]{2,1,0:T(8,128)(2,1)S(1)}, bf16[2,16,640]{2,1,0:T(8,128)(2,1)S(1)}, u32[]{:S(2)}, u32[]{:S(2)}) collective-permute-start(bf16[2,16,640]{2,1,0:T(8,128)(2,1)S(1)} %get-tuple-element.22), channel_id=1, source_target_pairs={{0,1},{1,0},{2,3},{3,2},{4,5},{5,4},{6,7},{7,6},{8,16},{9,17},{10,... | collective-permute-start | bytes 122888 | tf_op jit(solution)/shard_map/ppermute | solution.py:260

commit v2 on v1

v2 whole, which is shorter than its diff:
```python
import jax
import jax.numpy as jnp
from jax import lax
from jax.experimental import pallas as pl
from jax.experimental.pallas import tpu as pltpu
from jax.sharding import PartitionSpec as P

face_steps = ((0, 0), (-1, 0), (1, 0), (0, -1), (0, 1))
ROWS = 16
NT = (((1,), (1,)), ((), ()))
AXES = ("gx", "gy")


def exchange_pairs(count_x, count_y):
    spot = lambda x, y: x * count_y + y
    result = []
    for parity in (0, 1):
        pairs = []
        for x in range(count_x):
            other = x + 1 if (x % 2 == parity) else x - 1
            for y in range(count_y):
                inside = 0 <= other < count_x
                pairs.append((spot(x, y), spot(other, y) if inside else spot(x, y ^ 1)))
        result.append(pairs)
    for parity in (0, 1):
        pairs = []
        for y in range(count_y):
            other = y + 1 if (y % 2 == parity) else y - 1
            for x in range(count_x):
                inside = 0 <= other < count_y
                pairs.append((spot(x, y), spot(x, other) if inside else spot(x ^ 1, y)))
        result.append(pairs)
    return result


def place(axis):
    index = lax.axis_index(axis)
    even = lax.rem(index, 2) == 0
    return index, even


def run(body, inputs, spaces, outputs, scratch=(), cost=None, name=None):
    many = isinstance(outputs, (tuple, list))
    inside = pl.BlockSpec(memory_space=pltpu.VMEM)
    return pl.pallas_call(
        body,
        out_shape=outputs,
        in_specs=[pl.BlockSpec(memory_space=space) for space in spaces],
        out_specs=[inside] * len(outputs) if many else inside,
        scratch_shapes=list(scratch),
        compiler_params=pltpu.CompilerParams(vmem_limit_bytes=20 << 20),
        cost_estimate=cost,
        name=name,
    )(*inputs)


def packed(first, second):
    return first[:, :128], second[:, :128], jnp.concatenate([first[:, 128:], second[:, 128:]], axis=1)


def unpacked(wire, spot):
    half = wire.shape[-1] // 2
    rest = wire[spot // 2, 2]
    rest = rest[:, half:] if spot % 2 else rest[:, :half]
    return jnp.concatenate([wire[spot // 2, spot % 2], rest], axis=1)


def send_pairs(send, values):
    for pair in range(len(values) // 2):
        for part, value in enumerate(packed(values[2 * pair], values[2 * pair + 1])):
            send[pair, part] = value


def slots_kernel(codes_hbm, p_hbm, slots_ref, faces, send_a, send_b, codes, p_ref, arrived):
    tile_x, slots, unknowns, tile_y, edges = p_ref.shape
    _, even = place("gx")
    copies = [
        pltpu.make_async_copy(codes_hbm, codes, arrived.at[0]),
        pltpu.make_async_copy(p_hbm, p_ref, arrived.at[1]),
    ]
    for copy in copies:
        copy.start()
    faces[...] = jnp.zeros_like(faces)
    for copy in copies:
        copy.wait()
    pad = lax.broadcasted_iota(jnp.int32, (ROWS - unknowns, edges), 0) + 1
    for x in range(tile_x):
        for m in range(slots):
            rows = p_ref[x, m]
            for y in range(tile_y):
                code = codes[m, y, x]
                block = rows[:, y, :]
                faces[x, y, code, 0:unknowns, :] = block
                marks = jnp.where(pad == code, 1.0, 0.0).astype(jnp.bfloat16)
                slots_ref[x, y, m * ROWS : m * ROWS + unknowns, :] = block
                slots_ref[x, y, m * ROWS + unknowns : (m + 1) * ROWS, :] = marks
    for send, row in (
        (send_a, jnp.where(even, tile_x - 1, 0)),
        (send_b, jnp.where(even, 0, tile_x - 1)),
    ):
        send_pairs(send, [slots_ref[row, y] for y in range(tile_y)])


def x_side(got_a, got_b, y, even):
    from_a, from_b = unpacked(got_a, y), unpacked(got_b, y)
    return jnp.where(even, from_b, from_a), jnp.where(even, from_a, from_b)


def strips_kernel(slots_ref, got_a, got_b, send_a, send_b):
    tile_x, tile_y = slots_ref.shape[:2]
    _, even_x = place("gx")
    _, even_y = place("gy")
    first = x_side(got_a, got_b, 0, even_x)
    last = x_side(got_a, got_b, tile_y - 1, even_x)
    for send, upper in ((send_a, even_y), (send_b, jnp.logical_not(even_y))):
        column = jnp.where(upper, tile_y - 1, 0)
        ends = [jnp.where(upper, high, low) for low, high in zip(first, last)]
        middle = [slots_ref[x, column] for x in range(tile_x)]
        send_pairs(send, [ends[0], *middle, ends[1]])


def rows_kernel(slots_ref, a_hbm, result, a_ref, arrived):
    tile_x, tile_y, count = a_hbm.shape[:3]
    copies = {}
    for x in range(tile_x):
        for y in range(tile_y):
            copies[x, y] = pltpu.make_async_copy(
                a_hbm.at[x, y], a_ref.at[x, y], arrived.at[x * tile_y + y]
            )
            copies[x, y].start()
    for x in range(tile_x):
        for y in range(tile_y):
            copies[x, y].wait()
            for k in range(count):
                result[x, y, k] = jnp.dot(
                    slots_ref[x, y], a_ref[x, y, k], preferred_element_type=jnp.float32
                ).astype(result.dtype)


def terms_kernel(count_x, count_y, unknowns):
    span = 49 * unknowns
    lanes = -(-span // 128) * 128

    def body(
        a_hbm, p_hbm, u_ref, faces, got_xa, got_xb, got_ya, got_yb,
        own, send_xa, send_xb, send_ya, send_yb,
        a_codes, p_codes, near, summed, spread, total, arrived,
    ):
        tile_x, tile_y, slots, held, edges = u_ref.shape
        copies = [
            pltpu.make_async_copy(a_hbm, a_codes, arrived.at[0]),
            pltpu.make_async_copy(p_hbm, p_codes, arrived.at[1]),
        ]
        for copy in copies:
            copy.start()
        index_x, even_x = place("gx")
        index_y, even_y = place("gy")
        wide = tile_y + 2
        blank = (tile_x + 2) * wide
        near[blank] = jnp.zeros(near.shape[1:], near.dtype)

        def expand(spot, value, live):
            value = jnp.where(live, value, jnp.zeros_like(value))
            near[spot, 0:ROWS, :] = value[0:ROWS]
            for q in range(1, 5):
                block = jnp.zeros((ROWS, edges), near.dtype)
                for m in range(1, held // ROWS):
                    mark = value[m * ROWS + unknowns + q - 1 : m * ROWS + unknowns + q]
                    block += mark * value[m * ROWS : (m + 1) * ROWS]
                near[spot, q * ROWS : (q + 1) * ROWS, :] = block

        for y in range(tile_y):
            low, high = x_side(got_xa, got_xb, y, even_x)
            expand(1 + y, low, index_x > 0)
            expand((tile_x + 1) * wide + 1 + y, high, index_x < count_x - 1)
            for x in range(tile_x):
                near[(1 + x) * wide + 1 + y] = faces[x, y, 0:5].reshape(near.shape[1:])
        for x in range(tile_x + 2):
            from_a, from_b = unpacked(got_ya, x), unpacked(got_yb, x)
            inside = True
            if x == 0:
                inside = index_x > 0
            if x == tile_x + 1:
                inside = index_x < count_x - 1
            low, high = index_y > 0, index_y < count_y - 1
            expand(x * wide, jnp.where(even_y, from_b, from_a), jnp.logical_and(low, inside))
            expand(
                x * wide + wide - 1, jnp.where(even_y, from_a, from_b), jnp.logical_and(high, inside)
            )
        total[...] = jnp.zeros_like(total)
        spread[...] = jnp.zeros_like(spread)
        wing = lax.broadcasted_iota(jnp.int32, (ROWS, 128), 1) < 64
        row = lax.broadcasted_iota(jnp.int32, (held, 128), 0)
        lane = lax.broadcasted_iota(jnp.int32, (held, 128), 1)
        picks = jnp.where(jnp.logical_or(lane == row, lane == row + 64), 1.0, 0.0)
        picks = picks.astype(jnp.bfloat16)
        for copy in copies:
            copy.wait()
        for x in range(tile_x):
            for y in range(tile_y):
                turn = x * tile_y + y
                blocks = summed.at[turn % summed.shape[0]]
                blocks[...] = jnp.zeros(blocks.shape, blocks.dtype)
                for k in range(slots):
                    code = a_codes[x, y, k]
                    live = code < 9
                    step_x = lax.div(code, 3)
                    step_y = lax.rem(code, 3)
                    spot = jnp.where(live, (x + step_x) * wide + y + step_y, blank)
                    base = jnp.where(live, (step_x + 1) * 5 + step_y + 1, 12)
                    one = jnp.concatenate(
                        [u_ref[x, y, k], jnp.zeros((64 - held, edges), u_ref.dtype)], axis=0
                    )
                    product = lax.dot_general(
                        near[spot],
                        jnp.concatenate([one, one], axis=0),
                        NT,
                        preferred_element_type=jnp.float32,
                    )
                    for q, (face_x, face_y) in enumerate(face_steps):
                        blocks[base + face_x * 5 + face_y] += product[q * ROWS : (q + 1) * ROWS]
                stack = spread.at[turn % spread.shape[0]]
                for o in range(25):
                    value = blocks[o]
                    high = value.astype(jnp.bfloat16).astype(jnp.float32)
                    start = ((o // 5 + 1) * 7 + o % 5 + 1) * unknowns
                    stack[start : start + unknowns, :] = jnp.where(wing, high, value - high)[:unknowns]
                terms = lax.dot_general(
                    picks, stack[...].astype(jnp.bfloat16), NT, preferred_element_type=jnp.float32
                )
                for m in range(held // ROWS):
                    part = terms[m * ROWS : (m + 1) * ROWS]
                    spot = (1 + x) * wide + 1 + y
                    if m:
                        code = p_codes[m, y, x]
                        face_x = jnp.where(code == 1, -1, jnp.where(code == 2, 1, 0))
                        face_y = jnp.where(code == 3, -1, jnp.where(code == 4, 1, 0))
                        shift = (face_x * 7 + face_y) * unknowns
                        part = pltpu.roll(part, jnp.where(shift > 0, lanes - shift, -shift), 1)
                        spot = jnp.where(code < 5, spot + face_x * wide + face_y, blank)
                    total[spot] += part
        for x in range(tile_x):
            for y in range(tile_y):
                own[x, y] = total[(1 + x) * wide + 1 + y, 0:unknowns, 0:span]
        for send, far in ((send_xa, even_x), (send_xb, jnp.logical_not(even_x))):
            for y in range(tile_y):
                spot = jnp.where(far, (tile_x + 1) * wide, 0) + 1 + y
                send[y] = total[spot].astype(send.dtype)
        for send, far in ((send_ya, even_y), (send_yb, jnp.logical_not(even_y))):
            for x in range(tile_x):
                spot = (1 + x) * wide + jnp.where(far, wide - 1, 0)
                send[x] = total[spot].astype(send.dtype)

    return body


def sum_kernel(count_x, count_y):
    def body(own, got_xa, got_xb, got_ya, got_yb, result):
        tile_x, tile_y, unknowns, span = own.shape
        index_x, even_x = place("gx")
        index_y, even_y = place("gy")

        def shown(value, live):
            value = value[0:unknowns, 0:span].astype(jnp.float32)
            return jnp.where(live, value, jnp.zeros_like(value))

        low_x, high_x = index_x > 0, index_x < count_x - 1
        low_y, high_y = index_y > 0, index_y < count_y - 1
        for x in range(tile_x):
            for y in range(tile_y):
                value = own[x, y]
                if x == 0:
                    value += shown(jnp.where(even_x, got_xb[y], got_xa[y]), low_x)
                if x == tile_x - 1:
                    value += shown(jnp.where(even_x, got_xa[y], got_xb[y]), high_x)
                if y == 0:
                    value += shown(jnp.where(even_y, got_yb[x], got_ya[x]), low_y)
                if y == tile_y - 1:
                    value += shown(jnp.where(even_y, got_ya[x], got_yb[x]), high_y)
                result[x, :, y, :] = value

    return body


def solution(mesh):
    count_x, count_y = mesh.shape["gx"], mesh.shape["gy"]
    pairs = exchange_pairs(count_x, count_y)
    hbm, inside = pltpu.HBM, pltpu.VMEM

    def shards(a_blocks, a_codes, p_blocks, p_codes):
        tile_x, tile_y, slots, edges, _ = a_blocks.shape
        held, unknowns = p_blocks.shape[2:4]
        span = 49 * unknowns
        lanes = -(-span // 128) * 128
        half = lambda *dims: jax.ShapeDtypeStruct(dims, jnp.bfloat16)
        codes = jnp.transpose(p_codes, (2, 1, 0))
        blocks = jnp.transpose(p_blocks, (0, 2, 3, 1, 4))
        wire = (3, held * ROWS, 128)
        dma = pltpu.SemaphoreType.DMA
        slots_ref, faces, send_a, send_b = run(
            slots_kernel,
            (codes, blocks),
            (hbm, hbm),
            (
                half(tile_x, tile_y, held * ROWS, edges),
                half(tile_x, tile_y, 6, ROWS, edges),
                half(tile_y // 2, *wire),
                half(tile_y // 2, *wire),
            ),
            scratch=(
                pltpu.SMEM(codes.shape, codes.dtype),
                pltpu.VMEM(blocks.shape, blocks.dtype),
                dma((2,)),
            ),
            name="slots",
        )
        got_xa = lax.ppermute(send_a, AXES, pairs[0])
        got_xb = lax.ppermute(send_b, AXES, pairs[1])
        u_rows = run(
            rows_kernel,
            (slots_ref, a_blocks),
            (inside, hbm),
            half(tile_x, tile_y, slots, held * ROWS, edges),
            scratch=(pltpu.VMEM(a_blocks.shape, a_blocks.dtype), dma((tile_x * tile_y,))),
            cost=pl.CostEstimate(
                flops=2 * held * ROWS * a_blocks.size,
                bytes_accessed=2 * a_blocks.size,
                transcendentals=0,
            ),
            name="rows",
        )
        send_a, send_b = run(
            strips_kernel,
            (slots_ref, got_xa, got_xb),
            (inside,) * 3,
            (half(tile_x // 2 + 1, *wire), half(tile_x // 2 + 1, *wire)),
            name="strips",
        )
        got_ya = lax.ppermute(send_a, AXES, pairs[2])
        got_yb = lax.ppermute(send_b, AXES, pairs[3])
        ring = (tile_x + 2) * (tile_y + 2) + 1
        own, *sends = run(
            terms_kernel(count_x, count_y, unknowns),
            (a_codes, codes, u_rows, faces, got_xa, got_xb, got_ya, got_yb),
            (hbm, hbm) + (inside,) * 6,
            (
                jax.ShapeDtypeStruct((tile_x, tile_y, unknowns, span), jnp.float32),
                half(tile_y, ROWS, lanes),
                half(tile_y, ROWS, lanes),
                half(tile_x, ROWS, lanes),
                half(tile_x, ROWS, lanes),
            ),
            scratch=(
                pltpu.SMEM(a_codes.shape, a_codes.dtype),
                pltpu.SMEM(codes.shape, codes.dtype),
                pltpu.VMEM((ring, 5 * ROWS, edges), jnp.bfloat16),
                pltpu.VMEM((2, 25, ROWS, 128), jnp.float32),
                pltpu.VMEM((2, lanes, 128), jnp.float32),
                pltpu.VMEM((ring, ROWS, lanes), jnp.float32),
                dma((2,)),
            ),
            name="terms",
        )
        got = [lax.ppermute(send, AXES, p) for send, p in zip(sends, pairs)]
        result = run(
            sum_kernel(count_x, count_y),
            (own, *got),
            (inside,) * 5,
            jax.ShapeDtypeStruct((tile_x, unknowns, tile_y, span), jnp.float32),
            name="sum",
        )
        return jnp.transpose(result, (0, 2, 1, 3))

    in_specs = (
        P("gx", "gy", None, None, None),
        P("gx", "gy", None),
        P("gx", "gy", None, None, None),
        P("gx", "gy", None),
    )
    out_specs = P("gx", "gy", None, None)
    return jax.shard_map(shards, mesh=mesh, in_specs=in_specs, out_specs=out_specs, check_vma=False)
```

time: 31.5 us -> 29 us (0.921)
  the two profiles are of different devices: /device:TPU:0 before, /device:TPU:4 now
where the time goes in v2:
time: 29 us; the launch traced here: 28.9 us
  Pallas kernels  9.88 us (34%)
  waiting for transfers between devices  9.27 us (32%)
  starting transfers between devices  5.92 us (20%)
  local copies, waits for them, and re-layouts  3.71 us (13%)
    pallas_call x5, Pallas kernels, run(): pl.pallas_call(body, out_shape=outputs, in_specs=[pl.BlockSpec(memory_spa...  9.88 us
    ppermute x4, waiting for transfers between devices, shards(): got = [lax.ppermute(send, AXES, p) for send, p in zip(sends, pairs)]  4.43 us
    ppermute x4, starting transfers between devices, shards(): got = [lax.ppermute(send, AXES, p) for send, p in zip(sends, pairs)]  4.24 us
    unnamed x8, local copies, waits for them, and re-layouts  3.71 us
    ppermute x1, waiting for transfers between devices, shards(): got_xa = lax.ppermute(send_a, AXES, pairs[0])  2.45 us
    ppermute x1, waiting for transfers between devices, shards(): got_xb = lax.ppermute(send_b, AXES, pairs[1])  2.39 us
    ppermute x1, starting transfers between devices, shards(): got_xa = lax.ppermute(send_a, AXES, pairs[0])  1.55 us
  transfers between devices with their start and end apart: 8, of which 4 were waited for; matrix products, arithmetic and copies ran while one was open for 0% of the time, Pallas kernels for 15%

profile of v2, /device:TPU:4, one launch (start us, length us, event | category | flops | bytes accessed | tf_op | source)
XLA Modules:
  0.0 28.9 jit_solution(14742162566489647225)
XLA Ops:
  0.0 0.0 copy-start.1
  0.0 0.9 %copy-done.1 = bf16[4,2,3,12,192]{4,1,3,2,0:T(2,128)(2,1)S(1)} copy-done((bf16[4,2,3,12,192]{4,1,3,2,0:T(2,128)(2,1)S(1)}, bf16[4,2,3,12,192]{4,1,3,2,0:T(2,128)(2,1)}, u32[]{:S(2)}) %copy-start.1) | copy-done | bytes 110616
  0.9 0.0 copy-start.2
  0.9 0.7 %copy-done.2 = s32[4,2,3]{0,1,2:T(2,128)S(1)} copy-done((s32[4,2,3]{0,1,2:T(2,128)S(1)}, s32[4,2,3]{0,1,2:T(2,128)}, u32[]{:S(2)}) %copy-start.2) | copy-done | bytes 120
  1.6 0.0 copy-start.3
  1.6 0.9 %slots.1 = (bf16[4,2,48,192]{3,2,1,0:T(8,128)(2,1)S(1)}, bf16[4,2,6,16,192]{4,3,2,1,0:T(8,128)(2,1)S(1)}, bf16[1,3,48,128]{3,2,1,0:T(8,128)(2,1)S(1)}, bf16[1,3,48,128]{3,2,1,0:T(8,128)(2,1)S(1)}) custom-call(s32[3,2,4]{2,1,0:T(2,128)S(1)} %bitcast.4, bf16[4,3,12,2,192]{4,3,2,1,0:T(2,128)(2,1)S(1)} %bitcast.3), custom_call_target="tpu_custom_call" | custom-call | tf_op jit(solution)/shard_map/slots/pallas_call | solution.py:45
  2.5 1.6 %collective-permute-start = (bf16[1,3,48,128]{3,2,1,0:T(8,128)(2,1)S(1)}, bf16[1,3,48,128]{3,2,1,0:T(8,128)(2,1)S(1)}, u32[]{:S(2)}, u32[]{:S(2)}) collective-permute-start(bf16[1,3,48,128]{3,2,1,0:T(8,128)(2,1)S(1)} %get-tuple-element.18), channel_id=1, source_target_pairs={{0,8},{1,9},{2,10},{3,11},{4,12},{5,13},{6,14},{7,15},{8,0},{9,1},... | collective-permute-start | bytes 110600 | tf_op jit(solution)/shard_map/ppermute | solution.py:317
  4.1 0.0 collective-permute-start.1
  4.1 2.4 %collective-permute-done.got_a.got_xa = bf16[1,3,48,128]{3,2,1,0:T(8,128)(2,1)S(1)} collective-permute-done((bf16[1,3,48,128]{3,2,1,0:T(8,128)(2,1)S(1)}, bf16[1,3,48,128]{3,2,1,0:T(8,128)(2,1)S(1)}, u32[]{:S(2)}, u32[]{:S(2)}) %collective-permute-start) | collective-permute-done | bytes 36896 | tf_op jit(solution)/shard_map/ppermute | solution.py:317
  6.6 2.4 %collective-permute-done.1.got_b.got_xb = bf16[1,3,48,128]{3,2,1,0:T(8,128)(2,1)S(1)} collective-permute-done((bf16[1,3,48,128]{3,2,1,0:T(8,128)(2,1)S(1)}, bf16[1,3,48,128]{3,2,1,0:T(8,128)(2,1)S(1)}, u32[]{:S(2)}, u32[]{:S(2)}) %collective-permute-start.1) | collective-permute-done | bytes 36896 | tf_op jit(solution)/shard_map/ppermute | solution.py:318
  9.0 0.1 strips.1
  9.1 0.0 collective-permute-start.2
  9.1 0.1 collective-permute-start.3
  9.2 0.0 copy-start
  9.2 2.1 %copy-done = bf16[4,2,5,192,192]{4,3,2,1,0:T(8,128)(2,1)S(1)} copy-done((bf16[4,2,5,192,192]{4,3,2,1,0:T(8,128)(2,1)S(1)}, bf16[4,2,5,192,192]{4,3,2,1,0:T(8,128)(2,1)}, u32[]{:S(2)}) %copy-start) | copy-done | bytes 2949144
  11.3 4.3 %rows.1.u_ref = bf16[4,2,5,48,192]{4,3,2,1,0:T(8,128)(2,1)S(1)} custom-call(bf16[4,2,48,192]{3,2,1,0:T(8,128)(2,1)S(1)} %get-tuple-element.16.slots_ref, bf16[4,2,5,192,192]{4,3,2,1,0:T(8,128)(2,1)S(1)} %copy-done), custom_call_target="tpu_custom_call" | custom-call | flops 141557760 | bytes 2949120 | tf_op jit(solution)/shard_map/rows/pallas_call | solution.py:45
  15.7 0.0 collective-permute-done.2.got_ya
  15.7 0.0 collective-permute-done.3.got_yb
  15.7 0.0 copy-done.3
  15.7 3.6 %terms.1 = (f32[4,2,12,588]{3,2,1,0:T(8,128)S(1)}, bf16[2,16,640]{2,1,0:T(8,128)(2,1)S(1)}, bf16[2,16,640]{2,1,0:T(8,128)(2,1)S(1)}, bf16[4,16,640]{2,1,0:T(8,128)(2,1)S(1)}, bf16[4,16,640]{2,1,0:T(8,128)(2,1)S(1)}) custom-call(s32[4,2,5]{2,1,0:T(2,128)S(1)} %copy-done.3, s32[3,2,4]{2,1,0:T(2,128)S(1)} %bitcast.5, ...), custom_call_target="tpu_custom_call" | custom-call | tf_op jit(solution)/shard_map/terms/pallas_call | solution.py:45
  19.4 1.7 %collective-permute-start.6 = (bf16[4,16,640]{2,1,0:T(8,128)(2,1)S(1)}, bf16[4,16,640]{2,1,0:T(8,128)(2,1)S(1)}, u32[]{:S(2)}, u32[]{:S(2)}) collective-permute-start(bf16[4,16,640]{2,1,0:T(8,128)(2,1)S(1)} %get-tuple-element.25), channel_id=1, source_target_pairs={{0,1},{8,9},{16,17},{24,25},{1,0},{9,8},{17,16},{25,24},{2,3},{10,... | collective-permute-start | bytes 245768 | tf_op jit(solution)/shard_map/ppermute | solution.py:364
  21.1 0.4 %collective-permute-start.7 = (bf16[4,16,640]{2,1,0:T(8,128)(2,1)S(1)}, bf16[4,16,640]{2,1,0:T(8,128)(2,1)S(1)}, u32[]{:S(2)}, u32[]{:S(2)}) collective-permute-start(bf16[4,16,640]{2,1,0:T(8,128)(2,1)S(1)} %get-tuple-element.26), channel_id=1, source_target_pairs={{0,8},{8,0},{16,24},{24,16},{1,2},{9,10},{17,18},{25,26},{2,1},{10... | collective-permute-start | bytes 245768 | tf_op jit(solution)/shard_map/ppermute | solution.py:364
  21.5 1.6 %collective-permute-start.4 = (bf16[2,16,640]{2,1,0:T(8,128)(2,1)S(1)}, bf16[2,16,640]{2,1,0:T(8,128)(2,1)S(1)}, u32[]{:S(2)}, u32[]{:S(2)}) collective-permute-start(bf16[2,16,640]{2,1,0:T(8,128)(2,1)S(1)} %get-tuple-element.23), channel_id=1, source_target_pairs={{0,8},{1,9},{2,10},{3,11},{4,12},{5,13},{6,14},{7,15},{8,0},{9,1},... | collective-permute-start | bytes 122888 | tf_op jit(solution)/shard_map/ppermute | solution.py:364
  23.1 0.5 %collective-permute-start.5 = (bf16[2,16,640]{2,1,0:T(8,128)(2,1)S(1)}, bf16[2,16,640]{2,1,0:T(8,128)(2,1)S(1)}, u32[]{:S(2)}, u32[]{:S(2)}) collective-permute-start(bf16[2,16,640]{2,1,0:T(8,128)(2,1)S(1)} %get-tuple-element.24), channel_id=1, source_target_pairs={{0,1},{1,0},{2,3},{3,2},{4,5},{5,4},{6,7},{7,6},{8,16},{9,17},{10,... | collective-permute-start | bytes 122888 | tf_op jit(solution)/shard_map/ppermute | solution.py:364
  23.6 2.8 %collective-permute-done.4.got_xa = bf16[2,16,640]{2,1,0:T(8,128)(2,1)S(1)} collective-permute-done((bf16[2,16,640]{2,1,0:T(8,128)(2,1)S(1)}, bf16[2,16,640]{2,1,0:T(8,128)(2,1)S(1)}, u32[]{:S(2)}, u32[]{:S(2)}) %collective-permute-start.4) | collective-permute-done | bytes 40992 | tf_op jit(solution)/shard_map/ppermute | solution.py:364
  26.4 1.6 %collective-permute-done.5.got_xb = bf16[2,16,640]{2,1,0:T(8,128)(2,1)S(1)} collective-permute-done((bf16[2,16,640]{2,1,0:T(8,128)(2,1)S(1)}, bf16[2,16,640]{2,1,0:T(8,128)(2,1)S(1)}, u32[]{:S(2)}, u32[]{:S(2)}) %collective-permute-start.5) | collective-permute-done | bytes 40992 | tf_op jit(solution)/shard_map/ppermute | solution.py:364
  28.0 0.0 collective-permute-done.6.got_ya
  28.0 0.0 collective-permute-done.7.got_yb
  28.0 0.8 %sum.1 = f32[4,12,2,588]{3,2,1,0:T(2,128)} custom-call(f32[4,2,12,588]{3,2,1,0:T(8,128)S(1)} %get-tuple-element.22.own, bf16[2,16,640]{2,1,0:T(8,128)(2,1)S(1)} %collective-permute-done.4.got_xa, bf16[2,16,640]{2,1,0:T(8,128)(2,1)S(1)} %collective-permute-done.5.got_xb, bf16[4,16,640]{2,1,0:T(8,128)(2,1)S(1)} %collective-permute-done.6.got_ya, ...), custom_call_target="tpu_custom_call" | custom-call | tf_op jit(solution)/shard_map/sum/pallas_call | solution.py:45
Async XLA Ops:
  0.0 0.9 %copy-start.1 = (bf16[4,2,3,12,192]{4,1,3,2,0:T(2,128)(2,1)S(1)}, bf16[4,2,3,12,192]{4,1,3,2,0:T(2,128)(2,1)}, u32[]{:S(2)}) copy-start(bf16[4,2,3,12,192]{4,1,3,2,0:T(2,128)(2,1)} %param.6) | copy-start | bytes 331780
  0.9 0.7 %copy-start.2 = (s32[4,2,3]{0,1,2:T(2,128)S(1)}, s32[4,2,3]{0,1,2:T(2,128)}, u32[]{:S(2)}) copy-start(s32[4,2,3]{0,1,2:T(2,128)} %param.7) | copy-start | bytes 292
  1.6 14.1 %copy-start.3 = (s32[4,2,5]{2,1,0:T(2,128)S(1)}, s32[4,2,5]{2,1,0:T(2,128)}, u32[]{:S(2)}) copy-start(s32[4,2,5]{2,1,0:T(2,128)} %a_hbm.3) | copy-start | bytes 484
  2.5 4.0 %collective-permute-start = (bf16[1,3,48,128]{3,2,1,0:T(8,128)(2,1)S(1)}, bf16[1,3,48,128]{3,2,1,0:T(8,128)(2,1)S(1)}, u32[]{:S(2)}, u32[]{:S(2)}) collective-permute-start(bf16[1,3,48,128]{3,2,1,0:T(8,128)(2,1)S(1)} %get-tuple-element.18), channel_id=1, source_target_pairs={{0,8},{1,9},{2,10},{3,11},{4,12},{5,13},{6,14},{7,15},{8,0},{9,1},... | collective-permute-start | bytes 110600 | tf_op jit(solution)/shard_map/ppermute | solution.py:317
  4.1 4.9 %collective-permute-start.1 = (bf16[1,3,48,128]{3,2,1,0:T(8,128)(2,1)S(1)}, bf16[1,3,48,128]{3,2,1,0:T(8,128)(2,1)S(1)}, u32[]{:S(2)}, u32[]{:S(2)}) collective-permute-start(bf16[1,3,48,128]{3,2,1,0:T(8,128)(2,1)S(1)} %get-tuple-element.19), channel_id=1, source_target_pairs={{0,1},{1,0},{2,3},{3,2},{4,5},{5,4},{6,7},{7,6},{8,16},{9,17},{10,... | collective-permute-start | bytes 110600 | tf_op jit(solution)/shard_map/ppermute | solution.py:318
  9.1 6.6 %collective-permute-start.2 = (bf16[3,3,48,128]{3,2,1,0:T(8,128)(2,1)S(1)}, bf16[3,3,48,128]{3,2,1,0:T(8,128)(2,1)S(1)}, u32[]{:S(2)}, u32[]{:S(2)}) collective-permute-start(bf16[3,3,48,128]{3,2,1,0:T(8,128)(2,1)S(1)} %get-tuple-element.20), channel_id=1, source_target_pairs={{0,1},{8,9},{16,17},{24,25},{1,0},{9,8},{17,16},{25,24},{2,3},{10,... | collective-permute-start | bytes 331784 | tf_op jit(solution)/shard_map/ppermute | solution.py:339
  9.1 6.6 %collective-permute-start.3 = (bf16[3,3,48,128]{3,2,1,0:T(8,128)(2,1)S(1)}, bf16[3,3,48,128]{3,2,1,0:T(8,128)(2,1)S(1)}, u32[]{:S(2)}, u32[]{:S(2)}) collective-permute-start(bf16[3,3,48,128]{3,2,1,0:T(8,128)(2,1)S(1)} %get-tuple-element.21), channel_id=1, source_target_pairs={{0,8},{8,0},{16,24},{24,16},{1,2},{9,10},{17,18},{25,26},{2,1},{10... | collective-permute-start | bytes 331784 | tf_op jit(solution)/shard_map/ppermute | solution.py:340
  9.2 2.1 %copy-start = (bf16[4,2,5,192,192]{4,3,2,1,0:T(8,128)(2,1)S(1)}, bf16[4,2,5,192,192]{4,3,2,1,0:T(8,128)(2,1)}, u32[]{:S(2)}) copy-start(bf16[4,2,5,192,192]{4,3,2,1,0:T(8,128)(2,1)} %a_hbm.2) | copy-start | bytes 8847364
  19.4 8.7 %collective-permute-start.6 = (bf16[4,16,640]{2,1,0:T(8,128)(2,1)S(1)}, bf16[4,16,640]{2,1,0:T(8,128)(2,1)S(1)}, u32[]{:S(2)}, u32[]{:S(2)}) collective-permute-start(bf16[4,16,640]{2,1,0:T(8,128)(2,1)S(1)} %get-tuple-element.25), channel_id=1, source_target_pairs={{0,1},{8,9},{16,17},{24,25},{1,0},{9,8},{17,16},{25,24},{2,3},{10,... | collective-permute-start | bytes 245768 | tf_op jit(solution)/shard_map/ppermute | solution.py:364
  21.1 6.9 %collective-permute-start.7 = (bf16[4,16,640]{2,1,0:T(8,128)(2,1)S(1)}, bf16[4,16,640]{2,1,0:T(8,128)(2,1)S(1)}, u32[]{:S(2)}, u32[]{:S(2)}) collective-permute-start(bf16[4,16,640]{2,1,0:T(8,128)(2,1)S(1)} %get-tuple-element.26), channel_id=1, source_target_pairs={{0,8},{8,0},{16,24},{24,16},{1,2},{9,10},{17,18},{25,26},{2,1},{10... | collective-permute-start | bytes 245768 | tf_op jit(solution)/shard_map/ppermute | solution.py:364
  21.5 4.9 %collective-permute-start.4 = (bf16[2,16,640]{2,1,0:T(8,128)(2,1)S(1)}, bf16[2,16,640]{2,1,0:T(8,128)(2,1)S(1)}, u32[]{:S(2)}, u32[]{:S(2)}) collective-permute-start(bf16[2,16,640]{2,1,0:T(8,128)(2,1)S(1)} %get-tuple-element.23), channel_id=1, source_target_pairs={{0,8},{1,9},{2,10},{3,11},{4,12},{5,13},{6,14},{7,15},{8,0},{9,1},... | collective-permute-start | bytes 122888 | tf_op jit(solution)/shard_map/ppermute | solution.py:364
  23.1 4.9 %collective-permute-start.5 = (bf16[2,16,640]{2,1,0:T(8,128)(2,1)S(1)}, bf16[2,16,640]{2,1,0:T(8,128)(2,1)S(1)}, u32[]{:S(2)}, u32[]{:S(2)}) collective-permute-start(bf16[2,16,640]{2,1,0:T(8,128)(2,1)S(1)} %get-tuple-element.24), channel_id=1, source_target_pairs={{0,1},{1,0},{2,3},{3,2},{4,5},{5,4},{6,7},{7,6},{8,16},{9,17},{10,... | collective-permute-start | bytes 122888 | tf_op jit(solution)/shard_map/ppermute | solution.py:364

commit v3 on v2

--- a/solution.py
+++ b/solution.py
@@ -42,6 +42,10 @@
 def run(body, inputs, spaces, outputs, scratch=(), cost=None, name=None):
     many = isinstance(outputs, (tuple, list))
     inside = pl.BlockSpec(memory_space=pltpu.VMEM)
+    held = [
+        pltpu.with_memory_space_constraint(value, space) if space == pltpu.HBM else value
+        for value, space in zip(inputs, spaces)
+    ]
     return pl.pallas_call(
         body,
         out_shape=outputs,
@@ -51,7 +55,7 @@
         compiler_params=pltpu.CompilerParams(vmem_limit_bytes=20 << 20),
         cost_estimate=cost,
         name=name,
-    )(*inputs)
+    )(*held)
 
 
 def packed(first, second):

time: 29 us -> 24.7 us (0.85)
  local copies, waits for them, and re-layouts: 3.71 us -> 0 us
  waiting for transfers between devices: 9.27 us -> 11.2 us
  starting transfers between devices: 5.92 us -> 4.27 us
  Pallas kernels: 9.88 us -> 8.97 us
    unnamed x8 -> x0, local copies, waits for them, and re-layouts: 3.71 us -> none
    ppermute x1, waiting for transfers between devices: 0.01 us -> 1.83 us  [shards(): got_yb = lax.ppermute(send_b, AXES, pairs[3])]
    ppermute x4, starting transfers between devices: 4.24 us -> 2.6 us  [shards(): got = [lax.ppermute(send, AXES, p) for send, p in zip(sends, pairs)]]
    pallas_call x5, Pallas kernels: 9.88 us -> 8.97 us  [run(): pl.pallas_call(body, out_shape=outputs, in_specs=[pl.BlockSpec(memory_spa...]
  transfers between devices with their start and end apart: 8 -> 8, of which waited for: 4 -> 5; matrix products, arithmetic and copies ran while one was open for 0% -> 0% of each run, Pallas kernels for 15% -> 12%
where the time goes in v3:
time: 24.7 us; the launch traced here: 24.5 us
  waiting for transfers between devices  11.2 us (45%)
  Pallas kernels  8.97 us (36%)
  starting transfers between devices  4.27 us (17%)
    pallas_call x5, Pallas kernels, run(): pl.pallas_call(body, out_shape=outputs, in_specs=[pl.BlockSpec(memory_spa...  8.97 us
    ppermute x4, waiting for transfers between devices, shards(): got = [lax.ppermute(send, AXES, p) for send, p in zip(sends, pairs)]  4.51 us
    ppermute x4, starting transfers between devices, shards(): got = [lax.ppermute(send, AXES, p) for send, p in zip(sends, pairs)]  2.6 us
    ppermute x1, waiting for transfers between devices, shards(): got_xa = lax.ppermute(send_a, AXES, pairs[0])  2.45 us
    ppermute x1, waiting for transfers between devices, shards(): got_xb = lax.ppermute(send_b, AXES, pairs[1])  2.39 us
    ppermute x1, waiting for transfers between devices, shards(): got_yb = lax.ppermute(send_b, AXES, pairs[3])  1.83 us
    ppermute x1, starting transfers between devices, shards(): got_xa = lax.ppermute(send_a, AXES, pairs[0])  1.55 us
  transfers between devices with their start and end apart: 8, of which 5 were waited for; matrix products, arithmetic and copies ran while one was open for 0% of the time, Pallas kernels for 12%

profile of v3, /device:TPU:4, one launch (start us, length us, event | category | flops | bytes accessed | tf_op | source)
XLA Modules:
  0.0 24.5 jit_solution(2325191631433871508)
XLA Ops:
  0.0 1.3 %slots.1 = (bf16[4,2,48,192]{3,2,1,0:T(8,128)(2,1)S(1)}, bf16[4,2,6,16,192]{4,3,2,1,0:T(8,128)(2,1)S(1)}, bf16[1,3,48,128]{3,2,1,0:T(8,128)(2,1)S(1)}, bf16[1,3,48,128]{3,2,1,0:T(8,128)(2,1)S(1)}) custom-call(s32[3,2,4]{2,1,0:T(2,128)} %bitcast.4, bf16[4,3,12,2,192]{4,3,2,1,0:T(2,128)(2,1)} %bitcast.3), custom_call_target="tpu_custom_call" | custom-call | tf_op jit(solution)/shard_map/slots/pallas_call | solution.py:49
  1.3 1.6 %collective-permute-start = (bf16[1,3,48,128]{3,2,1,0:T(8,128)(2,1)S(1)}, bf16[1,3,48,128]{3,2,1,0:T(8,128)(2,1)S(1)}, u32[]{:S(2)}, u32[]{:S(2)}) collective-permute-start(bf16[1,3,48,128]{3,2,1,0:T(8,128)(2,1)S(1)} %get-tuple-element.18), channel_id=1, source_target_pairs={{0,8},{1,9},{2,10},{3,11},{4,12},{5,13},{6,14},{7,15},{8,0},{9,1},... | collective-permute-start | bytes 110600 | tf_op jit(solution)/shard_map/ppermute | solution.py:321
  2.8 0.0 collective-permute-start.1
  2.8 2.4 %collective-permute-done.got_a.got_xa = bf16[1,3,48,128]{3,2,1,0:T(8,128)(2,1)S(1)} collective-permute-done((bf16[1,3,48,128]{3,2,1,0:T(8,128)(2,1)S(1)}, bf16[1,3,48,128]{3,2,1,0:T(8,128)(2,1)S(1)}, u32[]{:S(2)}, u32[]{:S(2)}) %collective-permute-start) | collective-permute-done | bytes 36896 | tf_op jit(solution)/shard_map/ppermute | solution.py:321
  5.3 2.4 %collective-permute-done.1.got_b.got_xb = bf16[1,3,48,128]{3,2,1,0:T(8,128)(2,1)S(1)} collective-permute-done((bf16[1,3,48,128]{3,2,1,0:T(8,128)(2,1)S(1)}, bf16[1,3,48,128]{3,2,1,0:T(8,128)(2,1)S(1)}, u32[]{:S(2)}, u32[]{:S(2)}) %collective-permute-start.1) | collective-permute-done | bytes 36896 | tf_op jit(solution)/shard_map/ppermute | solution.py:322
  7.7 0.1 strips.1
  7.8 0.0 collective-permute-start.2
  7.9 0.1 collective-permute-start.3
  7.9 2.9 %rows.1.u_ref = bf16[4,2,5,48,192]{4,3,2,1,0:T(8,128)(2,1)S(1)} custom-call(bf16[4,2,48,192]{3,2,1,0:T(8,128)(2,1)S(1)} %get-tuple-element.16.slots_ref, bf16[4,2,5,192,192]{4,3,2,1,0:T(8,128)(2,1)} %a_hbm.2), custom_call_target="tpu_custom_call" | custom-call | flops 141557760 | bytes 2949120 | tf_op jit(solution)/shard_map/rows/pallas_call | solution.py:49
  10.8 0.0 collective-permute-done.2.got_ya
  10.8 1.8 %collective-permute-done.3.got_yb = bf16[3,3,48,128]{3,2,1,0:T(8,128)(2,1)S(1)} collective-permute-done((bf16[3,3,48,128]{3,2,1,0:T(8,128)(2,1)S(1)}, bf16[3,3,48,128]{3,2,1,0:T(8,128)(2,1)S(1)}, u32[]{:S(2)}, u32[]{:S(2)}) %collective-permute-start.3) | collective-permute-done | bytes 110624 | tf_op jit(solution)/shard_map/ppermute | solution.py:344
  12.7 3.9 %terms.1 = (f32[4,2,12,588]{3,2,1,0:T(8,128)S(1)}, bf16[2,16,640]{2,1,0:T(8,128)(2,1)S(1)}, bf16[2,16,640]{2,1,0:T(8,128)(2,1)S(1)}, bf16[4,16,640]{2,1,0:T(8,128)(2,1)S(1)}, bf16[4,16,640]{2,1,0:T(8,128)(2,1)S(1)}) custom-call(s32[4,2,5]{2,1,0:T(2,128)} %a_hbm.3, s32[3,2,4]{2,1,0:T(2,128)} %bitcast.5, bf16[4,2,5,48,192]{4,3,2,1,0:T(8,128)(2,1)S(1)} %rows.1.u_ref, ...), custom_call_target="tpu_custom_call" | custom-call | tf_op jit(solution)/shard_map/terms/pallas_call | solution.py:49
  16.5 0.2 collective-permute-start.6
  16.7 0.2 collective-permute-start.7
  16.9 1.9 %collective-permute-start.4 = (bf16[2,16,640]{2,1,0:T(8,128)(2,1)S(1)}, bf16[2,16,640]{2,1,0:T(8,128)(2,1)S(1)}, u32[]{:S(2)}, u32[]{:S(2)}) collective-permute-start(bf16[2,16,640]{2,1,0:T(8,128)(2,1)S(1)} %get-tuple-element.23), channel_id=1, source_target_pairs={{0,8},{1,9},{2,10},{3,11},{4,12},{5,13},{6,14},{7,15},{8,0},{9,1},... | collective-permute-start | bytes 122888 | tf_op jit(solution)/shard_map/ppermute | solution.py:368
  18.7 0.4 %collective-permute-start.5 = (bf16[2,16,640]{2,1,0:T(8,128)(2,1)S(1)}, bf16[2,16,640]{2,1,0:T(8,128)(2,1)S(1)}, u32[]{:S(2)}, u32[]{:S(2)}) collective-permute-start(bf16[2,16,640]{2,1,0:T(8,128)(2,1)S(1)} %get-tuple-element.24), channel_id=1, source_target_pairs={{0,1},{1,0},{2,3},{3,2},{4,5},{5,4},{6,7},{7,6},{8,16},{9,17},{10,... | collective-permute-start | bytes 122888 | tf_op jit(solution)/shard_map/ppermute | solution.py:368
  19.1 2.9 %collective-permute-done.4.got_xa = bf16[2,16,640]{2,1,0:T(8,128)(2,1)S(1)} collective-permute-done((bf16[2,16,640]{2,1,0:T(8,128)(2,1)S(1)}, bf16[2,16,640]{2,1,0:T(8,128)(2,1)S(1)}, u32[]{:S(2)}, u32[]{:S(2)}) %collective-permute-start.4) | collective-permute-done | bytes 40992 | tf_op jit(solution)/shard_map/ppermute | solution.py:368
  22.0 1.6 %collective-permute-done.5.got_xb = bf16[2,16,640]{2,1,0:T(8,128)(2,1)S(1)} collective-permute-done((bf16[2,16,640]{2,1,0:T(8,128)(2,1)S(1)}, bf16[2,16,640]{2,1,0:T(8,128)(2,1)S(1)}, u32[]{:S(2)}, u32[]{:S(2)}) %collective-permute-start.5) | collective-permute-done | bytes 40992 | tf_op jit(solution)/shard_map/ppermute | solution.py:368
  23.6 0.0 collective-permute-done.6.got_ya
  23.6 0.0 collective-permute-done.7.got_yb
  23.7 0.8 %sum.1 = f32[4,12,2,588]{3,2,1,0:T(2,128)} custom-call(f32[4,2,12,588]{3,2,1,0:T(8,128)S(1)} %get-tuple-element.22.own, bf16[2,16,640]{2,1,0:T(8,128)(2,1)S(1)} %collective-permute-done.4.got_xa, bf16[2,16,640]{2,1,0:T(8,128)(2,1)S(1)} %collective-permute-done.5.got_xb, bf16[4,16,640]{2,1,0:T(8,128)(2,1)S(1)} %collective-permute-done.6.got_ya, ...), custom_call_target="tpu_custom_call" | custom-call | tf_op jit(solution)/shard_map/sum/pallas_call | solution.py:49
Async XLA Ops:
  1.3 4.0 %collective-permute-start = (bf16[1,3,48,128]{3,2,1,0:T(8,128)(2,1)S(1)}, bf16[1,3,48,128]{3,2,1,0:T(8,128)(2,1)S(1)}, u32[]{:S(2)}, u32[]{:S(2)}) collective-permute-start(bf16[1,3,48,128]{3,2,1,0:T(8,128)(2,1)S(1)} %get-tuple-element.18), channel_id=1, source_target_pairs={{0,8},{1,9},{2,10},{3,11},{4,12},{5,13},{6,14},{7,15},{8,0},{9,1},... | collective-permute-start | bytes 110600 | tf_op jit(solution)/shard_map/ppermute | solution.py:321
  2.8 4.9 %collective-permute-start.1 = (bf16[1,3,48,128]{3,2,1,0:T(8,128)(2,1)S(1)}, bf16[1,3,48,128]{3,2,1,0:T(8,128)(2,1)S(1)}, u32[]{:S(2)}, u32[]{:S(2)}) collective-permute-start(bf16[1,3,48,128]{3,2,1,0:T(8,128)(2,1)S(1)} %get-tuple-element.19), channel_id=1, source_target_pairs={{0,1},{1,0},{2,3},{3,2},{4,5},{5,4},{6,7},{7,6},{8,16},{9,17},{10,... | collective-permute-start | bytes 110600 | tf_op jit(solution)/shard_map/ppermute | solution.py:322
  7.8 3.0 %collective-permute-start.2 = (bf16[3,3,48,128]{3,2,1,0:T(8,128)(2,1)S(1)}, bf16[3,3,48,128]{3,2,1,0:T(8,128)(2,1)S(1)}, u32[]{:S(2)}, u32[]{:S(2)}) collective-permute-start(bf16[3,3,48,128]{3,2,1,0:T(8,128)(2,1)S(1)} %get-tuple-element.20), channel_id=1, source_target_pairs={{0,1},{8,9},{16,17},{24,25},{1,0},{9,8},{17,16},{25,24},{2,3},{10,... | collective-permute-start | bytes 331784 | tf_op jit(solution)/shard_map/ppermute | solution.py:343
  7.9 4.8 %collective-permute-start.3 = (bf16[3,3,48,128]{3,2,1,0:T(8,128)(2,1)S(1)}, bf16[3,3,48,128]{3,2,1,0:T(8,128)(2,1)S(1)}, u32[]{:S(2)}, u32[]{:S(2)}) collective-permute-start(bf16[3,3,48,128]{3,2,1,0:T(8,128)(2,1)S(1)} %get-tuple-element.21), channel_id=1, source_target_pairs={{0,8},{8,0},{16,24},{24,16},{1,2},{9,10},{17,18},{25,26},{2,1},{10... | collective-permute-start | bytes 331784 | tf_op jit(solution)/shard_map/ppermute | solution.py:344
  16.5 7.1 %collective-permute-start.6 = (bf16[4,16,640]{2,1,0:T(8,128)(2,1)S(1)}, bf16[4,16,640]{2,1,0:T(8,128)(2,1)S(1)}, u32[]{:S(2)}, u32[]{:S(2)}) collective-permute-start(bf16[4,16,640]{2,1,0:T(8,128)(2,1)S(1)} %get-tuple-element.25), channel_id=1, source_target_pairs={{0,1},{8,9},{16,17},{24,25},{1,0},{9,8},{17,16},{25,24},{2,3},{10,... | collective-permute-start | bytes 245768 | tf_op jit(solution)/shard_map/ppermute | solution.py:368
  16.7 6.9 %collective-permute-start.7 = (bf16[4,16,640]{2,1,0:T(8,128)(2,1)S(1)}, bf16[4,16,640]{2,1,0:T(8,128)(2,1)S(1)}, u32[]{:S(2)}, u32[]{:S(2)}) collective-permute-start(bf16[4,16,640]{2,1,0:T(8,128)(2,1)S(1)} %get-tuple-element.26), channel_id=1, source_target_pairs={{0,8},{8,0},{16,24},{24,16},{1,2},{9,10},{17,18},{25,26},{2,1},{10... | collective-permute-start | bytes 245768 | tf_op jit(solution)/shard_map/ppermute | solution.py:368
  16.9 5.2 %collective-permute-start.4 = (bf16[2,16,640]{2,1,0:T(8,128)(2,1)S(1)}, bf16[2,16,640]{2,1,0:T(8,128)(2,1)S(1)}, u32[]{:S(2)}, u32[]{:S(2)}) collective-permute-start(bf16[2,16,640]{2,1,0:T(8,128)(2,1)S(1)} %get-tuple-element.23), channel_id=1, source_target_pairs={{0,8},{1,9},{2,10},{3,11},{4,12},{5,13},{6,14},{7,15},{8,0},{9,1},... | collective-permute-start | bytes 122888 | tf_op jit(solution)/shard_map/ppermute | solution.py:368
  18.7 4.9 %collective-permute-start.5 = (bf16[2,16,640]{2,1,0:T(8,128)(2,1)S(1)}, bf16[2,16,640]{2,1,0:T(8,128)(2,1)S(1)}, u32[]{:S(2)}, u32[]{:S(2)}) collective-permute-start(bf16[2,16,640]{2,1,0:T(8,128)(2,1)S(1)} %get-tuple-element.24), channel_id=1, source_target_pairs={{0,1},{1,0},{2,3},{3,2},{4,5},{5,4},{6,7},{7,6},{8,16},{9,17},{10,... | collective-permute-start | bytes 122888 | tf_op jit(solution)/shard_map/ppermute | solution.py:368

commit v4 on v3

v4 whole, which is shorter than its diff:
```python
import jax
import jax.numpy as jnp
from jax import lax
from jax.experimental import pallas as pl
from jax.experimental.pallas import tpu as pltpu
from jax.sharding import PartitionSpec as P

face_steps = ((0, 0), (-1, 0), (1, 0), (0, -1), (0, 1))
ROWS = 16
NT = (((1,), (1,)), ((), ()))
AXES = ("gx", "gy")


def exchange_pairs(count_x, count_y):
    spot = lambda x, y: x * count_y + y
    result = []
    for parity in (0, 1):
        pairs = []
        for x in range(count_x):
            other = x + 1 if (x % 2 == parity) else x - 1
            for y in range(count_y):
                inside = 0 <= other < count_x
                pairs.append((spot(x, y), spot(other, y) if inside else spot(x, y ^ 1)))
        result.append(pairs)
    for parity in (0, 1):
        pairs = []
        for y in range(count_y):
            other = y + 1 if (y % 2 == parity) else y - 1
            for x in range(count_x):
                inside = 0 <= other < count_y
                pairs.append((spot(x, y), spot(x, other) if inside else spot(x ^ 1, y)))
        result.append(pairs)
    return result


def place(axis):
    index = lax.axis_index(axis)
    even = lax.rem(index, 2) == 0
    return index, even


def run(body, inputs, spaces, outputs, scratch=(), cost=None, name=None):
    many = isinstance(outputs, (tuple, list))
    inside = pl.BlockSpec(memory_space=pltpu.VMEM)
    held = [
        pltpu.with_memory_space_constraint(value, space) if space == pltpu.HBM else value
        for value, space in zip(inputs, spaces)
    ]
    return pl.pallas_call(
        body,
        out_shape=outputs,
        in_specs=[pl.BlockSpec(memory_space=space) for space in spaces],
        out_specs=[inside] * len(outputs) if many else inside,
        scratch_shapes=list(scratch),
        compiler_params=pltpu.CompilerParams(vmem_limit_bytes=20 << 20),
        cost_estimate=cost,
        name=name,
    )(*held)


def packed(first, second):
    return first[:, :128], second[:, :128], jnp.concatenate([first[:, 128:], second[:, 128:]], axis=1)


def unpacked(wire, spot):
    half = wire.shape[-1] // 2
    rest = wire[spot // 2, 2]
    rest = rest[:, half:] if spot % 2 else rest[:, :half]
    return jnp.concatenate([wire[spot // 2, spot % 2], rest], axis=1)


def send_pairs(send, values):
    for pair in range(len(values) // 2):
        for part, value in enumerate(packed(values[2 * pair], values[2 * pair + 1])):
            send[pair, part] = value


def x_side(got_a, got_b, y, even):
    from_a, from_b = unpacked(got_a, y), unpacked(got_b, y)
    return jnp.where(even, from_b, from_a), jnp.where(even, from_a, from_b)


def strips_kernel(slots_ref, got_a, got_b, send_a, send_b):
    tile_x, tile_y = slots_ref.shape[:2]
    _, even_x = place("gx")
    _, even_y = place("gy")
    first = x_side(got_a, got_b, 0, even_x)
    last = x_side(got_a, got_b, tile_y - 1, even_x)
    for send, upper in ((send_a, even_y), (send_b, jnp.logical_not(even_y))):
        column = jnp.where(upper, tile_y - 1, 0)
        ends = [jnp.where(upper, high, low) for low, high in zip(first, last)]
        middle = [slots_ref[x, column] for x in range(tile_x)]
        send_pairs(send, [ends[0], *middle, ends[1]])


def slot_rows(p_row, m, y, code, pad):
    marks = jnp.where(pad == code, 1.0, 0.0).astype(jnp.bfloat16)
    return jnp.concatenate([p_row[:, y, :], marks], axis=0)


def pad_rows(unknowns, edges):
    return lax.broadcasted_iota(jnp.int32, (ROWS - unknowns, edges), 0) + 1


def edges_kernel(codes_hbm, p_hbm, send_a, send_b, codes, p_ref, arrived):
    tile_x, slots, unknowns, tile_y, edges = p_hbm.shape
    _, even = place("gx")
    rows = (jnp.where(even, tile_x - 1, 0), jnp.where(even, 0, tile_x - 1))
    copies = [pltpu.make_async_copy(codes_hbm, codes, arrived.at[2])]
    for i, row in enumerate(rows):
        copies.append(pltpu.make_async_copy(p_hbm.at[row], p_ref.at[i], arrived.at[i]))
    for copy in copies:
        copy.start()
    for copy in copies:
        copy.wait()
    pad = pad_rows(unknowns, edges)
    for i, (send, row) in enumerate(zip((send_a, send_b), rows)):
        values = [[] for _ in range(tile_y)]
        for m in range(slots):
            p_row = p_ref[i, m]
            for y in range(tile_y):
                values[y].append(slot_rows(p_row, m, y, codes[m, y, row], pad))
        send_pairs(send, [jnp.concatenate(value, axis=0) for value in values])


def start_rows(a_hbm, a_ref, arrived, first):
    copies = {}
    for x in range(a_ref.shape[0]):
        for y in range(a_ref.shape[1]):
            copies[x, y] = pltpu.make_async_copy(
                a_hbm.at[first + x, y], a_ref.at[x, y], arrived.at[x, y]
            )
            copies[x, y].start()
    return copies


def finish_rows(copies, slots_ref, a_ref, result, first):
    for (x, y), copy in copies.items():
        copy.wait()
        for k in range(a_ref.shape[2]):
            result[x, y, k] = jnp.dot(
                slots_ref[first + x, y], a_ref[x, y, k], preferred_element_type=jnp.float32
            ).astype(result.dtype)


def inner_kernel(codes_hbm, p_hbm, a_hbm, slots_ref, faces, result, codes, p_ref, a_ref, arrived, rows_arrived):
    tile_x, slots, unknowns, tile_y, edges = p_ref.shape
    copies = [
        pltpu.make_async_copy(codes_hbm, codes, arrived.at[0]),
        pltpu.make_async_copy(p_hbm, p_ref, arrived.at[1]),
    ]
    for copy in copies:
        copy.start()
    row_copies = start_rows(a_hbm, a_ref, rows_arrived, 0)
    faces[...] = jnp.zeros_like(faces)
    for copy in copies:
        copy.wait()
    pad = pad_rows(unknowns, edges)
    for x in range(tile_x):
        for m in range(slots):
            p_row = p_ref[x, m]
            for y in range(tile_y):
                code = codes[m, y, x]
                block = slot_rows(p_row, m, y, code, pad)
                faces[x, y, code] = block
                slots_ref[x, y, m * ROWS : (m + 1) * ROWS, :] = block
    finish_rows(row_copies, slots_ref, a_ref, result, 0)


def outer_kernel(count_x, unknowns):
    def body(slots_ref, got_xa, got_xb, a_hbm, result, sides, a_ref, rows_arrived):
        first = a_hbm.shape[0] - a_ref.shape[0]
        row_copies = start_rows(a_hbm, a_ref, rows_arrived, first)
        index, even = place("gx")
        for y in range(sides.shape[1]):
            low, high = x_side(got_xa, got_xb, y, even)
            expand(sides.at[0, y], low, index > 0, unknowns)
            expand(sides.at[1, y], high, index < count_x - 1, unknowns)
        finish_rows(row_copies, slots_ref, a_ref, result, first)

    return body


def expand(target, value, live, unknowns):
    edges = value.shape[1]
    value = jnp.where(live, value, jnp.zeros_like(value))
    target[0:ROWS, :] = value[0:ROWS]
    for q in range(1, 5):
        block = None
        for m in range(1, value.shape[0] // ROWS):
            mark = value[m * ROWS + unknowns + q - 1 : m * ROWS + unknowns + q]
            term = mark * value[m * ROWS : (m + 1) * ROWS]
            block = term if block is None else block + term
        target[q * ROWS : (q + 1) * ROWS, :] = block


def face_of(step):
    return face_steps.index(step) if step in face_steps else None


def terms_kernel(count_x, count_y, unknowns):
    span = 49 * unknowns
    lanes = -(-span // 128) * 128

    def body(
        a_hbm, p_hbm, u_first, u_last, faces, sides, got_ya, got_yb,
        own, send_xa, send_xb, send_ya, send_yb,
        a_codes, p_codes, slot_of, part_of, near, products, spread, parts, arrived,
    ):
        tile_x, tile_y = faces.shape[:2]
        slots, held, edges = u_first.shape[2:]
        half = u_first.shape[0]
        mine = [(x, y) for x in range(tile_x) for y in range(tile_y)]
        copies = [
            pltpu.make_async_copy(a_hbm, a_codes, arrived.at[0]),
            pltpu.make_async_copy(p_hbm, p_codes, arrived.at[1]),
        ]
        for copy in copies:
            copy.start()
        index_x, even_x = place("gx")
        index_y, even_y = place("gy")
        wide = tile_y + 2
        flat = near.shape[1:]
        count = held // ROWS
        for i in range(len(mine)):
            for d in range(9):
                slot_of[i, d] = slots
            for q in range(5):
                part_of[i, q] = len(mine) * count
            products[i, slots] = jnp.zeros(products.shape[2:], products.dtype)
        parts[len(mine) * count] = jnp.zeros(parts.shape[1:], parts.dtype)
        for y in range(tile_y):
            near[1 + y] = sides[0, y]
            near[(tile_x + 1) * wide + 1 + y] = sides[1, y]
            for x in range(tile_x):
                near[(1 + x) * wide + 1 + y] = faces[x, y, 0:5].reshape(flat)
        for x in range(tile_x + 2):
            from_a, from_b = unpacked(got_ya, x), unpacked(got_yb, x)
            low, high = index_y > 0, index_y < count_y - 1
            if x == 0:
                low, high = jnp.logical_and(low, index_x > 0), jnp.logical_and(high, index_x > 0)
            if x == tile_x + 1:
                inside = index_x < count_x - 1
                low, high = jnp.logical_and(low, inside), jnp.logical_and(high, inside)
            expand(near.at[x * wide], jnp.where(even_y, from_b, from_a), low, unknowns)
            expand(near.at[x * wide + wide - 1], jnp.where(even_y, from_a, from_b), high, unknowns)
        row = lax.broadcasted_iota(jnp.int32, (held, 128), 0)
        lane = lax.broadcasted_iota(jnp.int32, (held, 128), 1)
        picks = jnp.where(jnp.logical_or(lane == row, lane == row + 64), 1.0, 0.0)
        picks = picks.astype(jnp.bfloat16)
        wing = lax.broadcasted_iota(jnp.int32, (ROWS, 128), 1) < 64
        spread[...] = jnp.zeros_like(spread)
        for copy in copies:
            copy.wait()
        for i, (x, y) in enumerate(mine):
            for k in range(slots):
                slot_of[i, a_codes[x, y, k]] = k
            for m in range(1, count):
                part_of[i, p_codes[m, y, x]] = i * count + m
        gap = jnp.zeros((64 - held, edges), u_first.dtype)
        for k in range(slots):
            for i, (x, y) in enumerate(mine):
                code = jnp.minimum(a_codes[x, y, k], 8) if k else 4
                spot = (x + code // 3) * wide + y + code % 3
                if k:
                    step = lax.div(code, 3)
                    spot = (x + step) * wide + y + code - 3 * step
                one = u_first[x, y, k] if x < half else u_last[x - half, y, k]
                products[i, k] = lax.dot_general(
                    near[spot],
                    jnp.concatenate([one, gap, one, gap], axis=0),
                    NT,
                    preferred_element_type=jnp.float32,
                )
        for i in range(len(mine)):
            stack = spread.at[i % spread.shape[0]]
            found = [slot_of[i, d] if d != 4 else 0 for d in range(9)]
            for o in range(25):
                value = None
                for q, (face_x, face_y) in enumerate(face_steps):
                    step_x, step_y = o // 5 - 2 - face_x, o % 5 - 2 - face_y
                    if abs(step_x) > 1 or abs(step_y) > 1:
                        continue
                    slot = found[3 * step_x + step_y + 4]
                    term = products[i, slot, q * ROWS : (q + 1) * ROWS, :]
                    value = term if value is None else value + term
                if value is None:
                    continue
                high = value.astype(jnp.bfloat16).astype(jnp.float32)
                start = ((o // 5 + 1) * 7 + o % 5 + 1) * unknowns
                stack[start : start + unknowns, :] = jnp.where(wing, high, value - high)[:unknowns]
            terms = lax.dot_general(
                picks, stack[...].astype(jnp.bfloat16), NT, preferred_element_type=jnp.float32
            )
            for m in range(count):
                parts[i * count + m] = terms[m * ROWS : (m + 1) * ROWS]

        def part(x, y, q):
            shift = (face_steps[q][0] * 7 + face_steps[q][1]) * unknowns
            return pltpu.roll(parts[part_of[x * tile_y + y, q]], (-shift) % lanes, 1)

        for i, (x, y) in enumerate(mine):
            value = parts[i * count]
            for q in range(1, 5):
                from_x, from_y = x - face_steps[q][0], y - face_steps[q][1]
                if 0 <= from_x < tile_x and 0 <= from_y < tile_y:
                    value += part(from_x, from_y, q)
            own[x, y] = value[0:unknowns, 0:span]
        for y in range(tile_y):
            low, high = part(0, y, 1), part(tile_x - 1, y, 2)
            send_xa[y] = jnp.where(even_x, high, low).astype(send_xa.dtype)
            send_xb[y] = jnp.where(even_x, low, high).astype(send_xb.dtype)
        for x in range(tile_x):
            low, high = part(x, 0, 3), part(x, tile_y - 1, 4)
            send_ya[x] = jnp.where(even_y, high, low).astype(send_ya.dtype)
            send_yb[x] = jnp.where(even_y, low, high).astype(send_yb.dtype)

    return body


def sum_kernel(count_x, count_y):
    def body(own, got_xa, got_xb, got_ya, got_yb, result):
        tile_x, tile_y, unknowns, span = own.shape
        index_x, even_x = place("gx")
        index_y, even_y = place("gy")

        def shown(value, live):
            value = value[0:unknowns, 0:span].astype(jnp.float32)
            return jnp.where(live, value, jnp.zeros_like(value))

        low_x, high_x = index_x > 0, index_x < count_x - 1
        low_y, high_y = index_y > 0, index_y < count_y - 1
        for x in range(tile_x):
            for y in range(tile_y):
                value = own[x, y]
                if x == 0:
                    value += shown(jnp.where(even_x, got_xb[y], got_xa[y]), low_x)
                if x == tile_x - 1:
                    value += shown(jnp.where(even_x, got_xa[y], got_xb[y]), high_x)
                if y == 0:
                    value += shown(jnp.where(even_y, got_yb[x], got_ya[x]), low_y)
                if y == tile_y - 1:
                    value += shown(jnp.where(even_y, got_ya[x], got_yb[x]), high_y)
                result[x, :, y, :] = value

    return body


def solution(mesh):
    count_x, count_y = mesh.shape["gx"], mesh.shape["gy"]
    pairs = exchange_pairs(count_x, count_y)
    hbm, inside = pltpu.HBM, pltpu.VMEM

    def shards(a_blocks, a_codes, p_blocks, p_codes):
        tile_x, tile_y, slots, edges, _ = a_blocks.shape
        held, unknowns = p_blocks.shape[2:4]
        span = 49 * unknowns
        lanes = -(-span // 128) * 128
        half = lambda *dims: jax.ShapeDtypeStruct(dims, jnp.bfloat16)
        codes = jnp.transpose(p_codes, (2, 1, 0))
        blocks = jnp.transpose(p_blocks, (0, 2, 3, 1, 4))
        wire = (3, held * ROWS, 128)
        dma = pltpu.SemaphoreType.DMA
        send_a, send_b = run(
            edges_kernel,
            (codes, blocks),
            (hbm, hbm),
            (half(tile_y // 2, *wire), half(tile_y // 2, *wire)),
            scratch=(
                pltpu.SMEM(codes.shape, codes.dtype),
                pltpu.VMEM((2, *blocks.shape[1:]), blocks.dtype),
                dma((3,)),
            ),
            name="edges",
        )
        got_xa = lax.ppermute(send_a, AXES, pairs[0])
        got_xb = lax.ppermute(send_b, AXES, pairs[1])
        early = tile_x // 2
        late = tile_x - early
        row_cost = lambda rows: pl.CostEstimate(
            flops=2 * held * ROWS * rows * (a_blocks.size // tile_x),
            bytes_accessed=2 * rows * (a_blocks.size // tile_x),
            transcendentals=0,
        )
        slots_ref, faces, u_first = run(
            inner_kernel,
            (codes, blocks, a_blocks),
            (hbm, hbm, hbm),
            (
                half(tile_x, tile_y, held * ROWS, edges),
                half(tile_x, tile_y, 6, ROWS, edges),
                half(early, tile_y, slots, held * ROWS, edges),
            ),
            scratch=(
                pltpu.SMEM(codes.shape, codes.dtype),
                pltpu.VMEM(blocks.shape, blocks.dtype),
                pltpu.VMEM((early, *a_blocks.shape[1:]), a_blocks.dtype),
                dma((2,)),
                dma((early, tile_y)),
            ),
            cost=row_cost(early),
            name="inner",
        )
        send_a, send_b = run(
            strips_kernel,
            (slots_ref, got_xa, got_xb),
            (inside,) * 3,
            (half(tile_x // 2 + 1, *wire), half(tile_x // 2 + 1, *wire)),
            name="strips",
        )
        got_ya = lax.ppermute(send_a, AXES, pairs[2])
        got_yb = lax.ppermute(send_b, AXES, pairs[3])
        u_last, sides = run(
            outer_kernel(count_x, unknowns),
            (slots_ref, got_xa, got_xb, a_blocks),
            (inside, inside, inside, hbm),
            (
                half(late, tile_y, slots, held * ROWS, edges),
                half(2, tile_y, 5 * ROWS, edges),
            ),
            scratch=(
                pltpu.VMEM((late, *a_blocks.shape[1:]), a_blocks.dtype),
                dma((late, tile_y)),
            ),
            cost=row_cost(late),
            name="outer",
        )
        amount = tile_x * tile_y
        own, *sends = run(
            terms_kernel(count_x, count_y, unknowns),
            (a_codes, codes, u_first, u_last, faces, sides, got_ya, got_yb),
            (hbm, hbm) + (inside,) * 6,
            (
                jax.ShapeDtypeStruct((tile_x, tile_y, unknowns, span), jnp.float32),
                half(tile_y, ROWS, lanes),
                half(tile_y, ROWS, lanes),
                half(tile_x, ROWS, lanes),
                half(tile_x, ROWS, lanes),
            ),
            scratch=(
                pltpu.SMEM(a_codes.shape, a_codes.dtype),
                pltpu.SMEM(codes.shape, codes.dtype),
                pltpu.SMEM((amount, 10), jnp.int32),
                pltpu.SMEM((amount, 6), jnp.int32),
                pltpu.VMEM(((tile_x + 2) * (tile_y + 2), 5 * ROWS, edges), jnp.bfloat16),
                pltpu.VMEM((amount, slots + 1, 5 * ROWS, 128), jnp.float32),
                pltpu.VMEM((4, lanes, 128), jnp.float32),
                pltpu.VMEM((amount * held + 1, ROWS, lanes), jnp.float32),
                dma((2,)),
            ),
            name="terms",
        )
        got = [lax.ppermute(send, AXES, p) for send, p in zip(sends, pairs)]
        result = run(
            sum_kernel(count_x, count_y),
            (own, *got),
            (inside,) * 5,
            jax.ShapeDtypeStruct((tile_x, unknowns, tile_y, span), jnp.float32),
            name="sum",
        )
        return jnp.transpose(result, (0, 2, 1, 3))

    in_specs = (
        P("gx", "gy", None, None, None),
        P("gx", "gy", None),
        P("gx", "gy", None, None, None),
        P("gx", "gy", None),
    )
    out_specs = P("gx", "gy", None, None)
    return jax.shard_map(shards, mesh=mesh, in_specs=in_specs, out_specs=out_specs, check_vma=False)
```

time: 24.7 us -> 23.4 us (0.947)
  waiting for transfers between devices: 11.2 us -> 9.17 us
  Pallas kernels: 8.97 us -> 9.32 us
  starting transfers between devices: 4.27 us -> 4.57 us
    ppermute x1, waiting for transfers between devices: 2.45 us -> 0.01 us  [shards(): got_xa = lax.ppermute(send_a, AXES, pairs[0])]
    ppermute x1, waiting for transfers between devices: 1.83 us -> 2.76 us  [shards(): got_yb = lax.ppermute(send_b, AXES, pairs[3])]
    pallas_call x5 -> x6, Pallas kernels: 8.97 us -> 9.32 us  [run(): pl.pallas_call(body, out_shape=outputs, in_specs=[pl.BlockSpec(memory_spa...]
    ppermute x4, waiting for transfers between devices: 4.51 us -> 4.19 us  [shards(): got = [lax.ppermute(send, AXES, p) for send, p in zip(sends, pairs)]]
    ppermute x4, starting transfers between devices: 2.6 us -> 2.9 us  [shards(): got = [lax.ppermute(send, AXES, p) for send, p in zip(sends, pairs)]]
  transfers between devices with their start and end apart: 8 -> 8, of which waited for: 5 -> 4; matrix products, arithmetic and copies ran while one was open for 0% -> 0% of each run, Pallas kernels for 12% -> 20%
where the time goes in v4:
time: 23.4 us; the launch traced here: 23.1 us
  Pallas kernels  9.32 us (40%)
  waiting for transfers between devices  9.17 us (39%)
  starting transfers between devices  4.57 us (20%)
    pallas_call x6, Pallas kernels, run(): pl.pallas_call(body, out_shape=outputs, in_specs=[pl.BlockSpec(memory_spa...  9.32 us
    ppermute x4, waiting for transfers between devices, shards(): got = [lax.ppermute(send, AXES, p) for send, p in zip(sends, pairs)]  4.19 us
    ppermute x4, starting transfers between devices, shards(): got = [lax.ppermute(send, AXES, p) for send, p in zip(sends, pairs)]  2.9 us
    ppermute x1, waiting for transfers between devices, shards(): got_yb = lax.ppermute(send_b, AXES, pairs[3])  2.76 us
    ppermute x1, waiting for transfers between devices, shards(): got_xb = lax.ppermute(send_b, AXES, pairs[1])  2.22 us
    ppermute x1, starting transfers between devices, shards(): got_xa = lax.ppermute(send_a, AXES, pairs[0])  1.56 us
  transfers between devices with their start and end apart: 8, of which 4 were waited for; matrix products, arithmetic and copies ran while one was open for 0% of the time, Pallas kernels for 20%

profile of v4, /device:TPU:4, one launch (start us, length us, event | category | flops | bytes accessed | tf_op | source)
XLA Modules:
  0.0 23.1 jit_solution(13169949902375281916)
XLA Ops:
  0.0 1.0 %edges.1 = (bf16[1,3,48,128]{3,2,1,0:T(8,128)(2,1)S(1)}, bf16[1,3,48,128]{3,2,1,0:T(8,128)(2,1)S(1)}) custom-call(s32[3,2,4]{2,1,0:T(2,128)} %bitcast.5, bf16[4,3,12,2,192]{4,3,2,1,0:T(2,128)(2,1)} %bitcast.3), custom_call_target="tpu_custom_call" | custom-call | tf_op jit(solution)/shard_map/edges/pallas_call | solution.py:49
  1.0 1.6 %collective-permute-start = (bf16[1,3,48,128]{3,2,1,0:T(8,128)(2,1)S(1)}, bf16[1,3,48,128]{3,2,1,0:T(8,128)(2,1)S(1)}, u32[]{:S(2)}, u32[]{:S(2)}) collective-permute-start(bf16[1,3,48,128]{3,2,1,0:T(8,128)(2,1)S(1)} %get-tuple-element.21), channel_id=1, source_target_pairs={{0,8},{1,9},{2,10},{3,11},{4,12},{5,13},{6,14},{7,15},{8,0},{9,1},... | collective-permute-start | bytes 110600 | tf_op jit(solution)/shard_map/ppermute | solution.py:376
  2.6 0.0 collective-permute-start.1
  2.6 2.6 %inner.1 = (bf16[4,2,48,192]{3,2,1,0:T(8,128)(2,1)S(1)}, bf16[4,2,6,16,192]{4,3,2,1,0:T(8,128)(2,1)S(1)}, bf16[2,2,5,48,192]{4,3,2,1,0:T(8,128)(2,1)S(1)}) custom-call(s32[3,2,4]{2,1,0:T(2,128)} %bitcast.6, bf16[4,3,12,2,192]{4,3,2,1,0:T(2,128)(2,1)} %bitcast.4, bf16[4,2,5,192,192]{4,3,2,1,0:T(8,128)(2,1)} %a_hbm.4), custom_call_target="tpu_custom_call" | custom-call | flops 70778880 | bytes 1474560 | tf_op jit(solution)/shard_map/inner/pallas_call | solution.py:49
  5.2 0.0 collective-permute-done.got_xa.got_a
  5.2 2.2 %collective-permute-done.1.got_xb.got_b = bf16[1,3,48,128]{3,2,1,0:T(8,128)(2,1)S(1)} collective-permute-done((bf16[1,3,48,128]{3,2,1,0:T(8,128)(2,1)S(1)}, bf16[1,3,48,128]{3,2,1,0:T(8,128)(2,1)S(1)}, u32[]{:S(2)}, u32[]{:S(2)}) %collective-permute-start.1) | collective-permute-done | bytes 36896 | tf_op jit(solution)/shard_map/ppermute | solution.py:377
  7.4 0.1 strips.1
  7.6 0.0 collective-permute-start.2
  7.6 0.1 collective-permute-start.3
  7.7 2.0 %outer.1 = (bf16[2,2,5,48,192]{4,3,2,1,0:T(8,128)(2,1)S(1)}, bf16[2,2,80,192]{3,2,1,0:T(8,128)(2,1)S(1)}) custom-call(bf16[4,2,48,192]{3,2,1,0:T(8,128)(2,1)S(1)} %get-tuple-element.20.slots_ref, bf16[1,3,48,128]{3,2,1,0:T(8,128)(2,1)S(1)} %collective-permute-done.got_xa.got_a, bf16[1,3,48,128]{3,2,1,0:T(8,128)(2,1)S(1)} %collective-permute-done.1.got_xb.got_b, ...), custom_call_target="tpu_custom_call" | custom-call | flops 70778880 | bytes 1474560 | tf_op jit(solution)/shard_map/outer/pallas_call | solution.py:49
  9.6 0.0 collective-permute-done.2.got_ya
  9.7 2.8 %collective-permute-done.3.got_yb = bf16[3,3,48,128]{3,2,1,0:T(8,128)(2,1)S(1)} collective-permute-done((bf16[3,3,48,128]{3,2,1,0:T(8,128)(2,1)S(1)}, bf16[3,3,48,128]{3,2,1,0:T(8,128)(2,1)S(1)}, u32[]{:S(2)}, u32[]{:S(2)}) %collective-permute-start.3) | collective-permute-done | bytes 110624 | tf_op jit(solution)/shard_map/ppermute | solution.py:412
  12.4 2.8 %terms.1 = (f32[4,2,12,588]{3,2,1,0:T(8,128)S(1)}, bf16[2,16,640]{2,1,0:T(8,128)(2,1)S(1)}, bf16[2,16,640]{2,1,0:T(8,128)(2,1)S(1)}, bf16[4,16,640]{2,1,0:T(8,128)(2,1)S(1)}, bf16[4,16,640]{2,1,0:T(8,128)(2,1)S(1)}) custom-call(s32[4,2,5]{2,1,0:T(2,128)} %a_hbm.5, s32[3,2,4]{2,1,0:T(2,128)} %bitcast.7, ...), custom_call_target="tpu_custom_call" | custom-call | tf_op jit(solution)/shard_map/terms/pallas_call | solution.py:49
  15.2 0.2 collective-permute-start.6
  15.4 0.0 collective-permute-start.7
  15.4 2.0 %collective-permute-start.4 = (bf16[2,16,640]{2,1,0:T(8,128)(2,1)S(1)}, bf16[2,16,640]{2,1,0:T(8,128)(2,1)S(1)}, u32[]{:S(2)}, u32[]{:S(2)}) collective-permute-start(bf16[2,16,640]{2,1,0:T(8,128)(2,1)S(1)} %get-tuple-element.29), channel_id=1, source_target_pairs={{0,8},{1,9},{2,10},{3,11},{4,12},{5,13},{6,14},{7,15},{8,0},{9,1},... | collective-permute-start | bytes 122888 | tf_op jit(solution)/shard_map/ppermute | solution.py:453
  17.4 0.7 %collective-permute-start.5 = (bf16[2,16,640]{2,1,0:T(8,128)(2,1)S(1)}, bf16[2,16,640]{2,1,0:T(8,128)(2,1)S(1)}, u32[]{:S(2)}, u32[]{:S(2)}) collective-permute-start(bf16[2,16,640]{2,1,0:T(8,128)(2,1)S(1)} %get-tuple-element.30), channel_id=1, source_target_pairs={{0,1},{1,0},{2,3},{3,2},{4,5},{5,4},{6,7},{7,6},{8,16},{9,17},{10,... | collective-permute-start | bytes 122888 | tf_op jit(solution)/shard_map/ppermute | solution.py:453
  18.1 2.6 %collective-permute-done.4.got_xa = bf16[2,16,640]{2,1,0:T(8,128)(2,1)S(1)} collective-permute-done((bf16[2,16,640]{2,1,0:T(8,128)(2,1)S(1)}, bf16[2,16,640]{2,1,0:T(8,128)(2,1)S(1)}, u32[]{:S(2)}, u32[]{:S(2)}) %collective-permute-start.4) | collective-permute-done | bytes 40992 | tf_op jit(solution)/shard_map/ppermute | solution.py:453
  20.7 1.6 %collective-permute-done.5.got_xb = bf16[2,16,640]{2,1,0:T(8,128)(2,1)S(1)} collective-permute-done((bf16[2,16,640]{2,1,0:T(8,128)(2,1)S(1)}, bf16[2,16,640]{2,1,0:T(8,128)(2,1)S(1)}, u32[]{:S(2)}, u32[]{:S(2)}) %collective-permute-start.5) | collective-permute-done | bytes 40992 | tf_op jit(solution)/shard_map/ppermute | solution.py:453
  22.3 0.0 collective-permute-done.6.got_ya
  22.3 0.0 collective-permute-done.7.got_yb
  22.3 0.8 %sum.1 = f32[4,12,2,588]{3,2,1,0:T(2,128)} custom-call(f32[4,2,12,588]{3,2,1,0:T(8,128)S(1)} %get-tuple-element.28.own, bf16[2,16,640]{2,1,0:T(8,128)(2,1)S(1)} %collective-permute-done.4.got_xa, bf16[2,16,640]{2,1,0:T(8,128)(2,1)S(1)} %collective-permute-done.5.got_xb, bf16[4,16,640]{2,1,0:T(8,128)(2,1)S(1)} %collective-permute-done.6.got_ya, ...), custom_call_target="tpu_custom_call" | custom-call | tf_op jit(solution)/shard_map/sum/pallas_call | solution.py:49
Async XLA Ops:
  1.0 4.2 %collective-permute-start = (bf16[1,3,48,128]{3,2,1,0:T(8,128)(2,1)S(1)}, bf16[1,3,48,128]{3,2,1,0:T(8,128)(2,1)S(1)}, u32[]{:S(2)}, u32[]{:S(2)}) collective-permute-start(bf16[1,3,48,128]{3,2,1,0:T(8,128)(2,1)S(1)} %get-tuple-element.21), channel_id=1, source_target_pairs={{0,8},{1,9},{2,10},{3,11},{4,12},{5,13},{6,14},{7,15},{8,0},{9,1},... | collective-permute-start | bytes 110600 | tf_op jit(solution)/shard_map/ppermute | solution.py:376
  2.6 4.9 %collective-permute-start.1 = (bf16[1,3,48,128]{3,2,1,0:T(8,128)(2,1)S(1)}, bf16[1,3,48,128]{3,2,1,0:T(8,128)(2,1)S(1)}, u32[]{:S(2)}, u32[]{:S(2)}) collective-permute-start(bf16[1,3,48,128]{3,2,1,0:T(8,128)(2,1)S(1)} %get-tuple-element.22), channel_id=1, source_target_pairs={{0,1},{1,0},{2,3},{3,2},{4,5},{5,4},{6,7},{7,6},{8,16},{9,17},{10,... | collective-permute-start | bytes 110600 | tf_op jit(solution)/shard_map/ppermute | solution.py:377
  7.6 2.1 %collective-permute-start.2 = (bf16[3,3,48,128]{3,2,1,0:T(8,128)(2,1)S(1)}, bf16[3,3,48,128]{3,2,1,0:T(8,128)(2,1)S(1)}, u32[]{:S(2)}, u32[]{:S(2)}) collective-permute-start(bf16[3,3,48,128]{3,2,1,0:T(8,128)(2,1)S(1)} %get-tuple-element.26), channel_id=1, source_target_pairs={{0,1},{8,9},{16,17},{24,25},{1,0},{9,8},{17,16},{25,24},{2,3},{10,... | collective-permute-start | bytes 331784 | tf_op jit(solution)/shard_map/ppermute | solution.py:411
  7.6 4.8 %collective-permute-start.3 = (bf16[3,3,48,128]{3,2,1,0:T(8,128)(2,1)S(1)}, bf16[3,3,48,128]{3,2,1,0:T(8,128)(2,1)S(1)}, u32[]{:S(2)}, u32[]{:S(2)}) collective-permute-start(bf16[3,3,48,128]{3,2,1,0:T(8,128)(2,1)S(1)} %get-tuple-element.27), channel_id=1, source_target_pairs={{0,8},{8,0},{16,24},{24,16},{1,2},{9,10},{17,18},{25,26},{2,1},{10... | collective-permute-start | bytes 331784 | tf_op jit(solution)/shard_map/ppermute | solution.py:412
  15.2 7.1 %collective-permute-start.6 = (bf16[4,16,640]{2,1,0:T(8,128)(2,1)S(1)}, bf16[4,16,640]{2,1,0:T(8,128)(2,1)S(1)}, u32[]{:S(2)}, u32[]{:S(2)}) collective-permute-start(bf16[4,16,640]{2,1,0:T(8,128)(2,1)S(1)} %get-tuple-element.31), channel_id=1, source_target_pairs={{0,1},{8,9},{16,17},{24,25},{1,0},{9,8},{17,16},{25,24},{2,3},{10,... | collective-permute-start | bytes 245768 | tf_op jit(solution)/shard_map/ppermute | solution.py:453
  15.4 6.9 %collective-permute-start.7 = (bf16[4,16,640]{2,1,0:T(8,128)(2,1)S(1)}, bf16[4,16,640]{2,1,0:T(8,128)(2,1)S(1)}, u32[]{:S(2)}, u32[]{:S(2)}) collective-permute-start(bf16[4,16,640]{2,1,0:T(8,128)(2,1)S(1)} %get-tuple-element.32), channel_id=1, source_target_pairs={{0,8},{8,0},{16,24},{24,16},{1,2},{9,10},{17,18},{25,26},{2,1},{10... | collective-permute-start | bytes 245768 | tf_op jit(solution)/shard_map/ppermute | solution.py:453
  15.4 5.3 %collective-permute-start.4 = (bf16[2,16,640]{2,1,0:T(8,128)(2,1)S(1)}, bf16[2,16,640]{2,1,0:T(8,128)(2,1)S(1)}, u32[]{:S(2)}, u32[]{:S(2)}) collective-permute-start(bf16[2,16,640]{2,1,0:T(8,128)(2,1)S(1)} %get-tuple-element.29), channel_id=1, source_target_pairs={{0,8},{1,9},{2,10},{3,11},{4,12},{5,13},{6,14},{7,15},{8,0},{9,1},... | collective-permute-start | bytes 122888 | tf_op jit(solution)/shard_map/ppermute | solution.py:453
  17.4 4.9 %collective-permute-start.5 = (bf16[2,16,640]{2,1,0:T(8,128)(2,1)S(1)}, bf16[2,16,640]{2,1,0:T(8,128)(2,1)S(1)}, u32[]{:S(2)}, u32[]{:S(2)}) collective-permute-start(bf16[2,16,640]{2,1,0:T(8,128)(2,1)S(1)} %get-tuple-element.30), channel_id=1, source_target_pairs={{0,1},{1,0},{2,3},{3,2},{4,5},{5,4},{6,7},{7,6},{8,16},{9,17},{10,... | collective-permute-start | bytes 122888 | tf_op jit(solution)/shard_map/ppermute | solution.py:453

commit v5 on v4

--- a/solution.py
+++ b/solution.py
@@ -124,26 +124,24 @@
 
 
 def start_rows(a_hbm, a_ref, arrived, first):
-    copies = {}
+    copies = []
     for x in range(a_ref.shape[0]):
+        copies.append(pltpu.make_async_copy(a_hbm.at[first + x], a_ref.at[x], arrived.at[x]))
+        copies[x].start()
+    return copies
+
+
+def finish_rows(copies, slots_ref, a_ref, result, first):
+    for x, copy in enumerate(copies):
+        copy.wait()
         for y in range(a_ref.shape[1]):
-            copies[x, y] = pltpu.make_async_copy(
-                a_hbm.at[first + x, y], a_ref.at[x, y], arrived.at[x, y]
-            )
-            copies[x, y].start()
-    return copies
-
-
-def finish_rows(copies, slots_ref, a_ref, result, first):
-    for (x, y), copy in copies.items():
-        copy.wait()
-        for k in range(a_ref.shape[2]):
-            result[x, y, k] = jnp.dot(
-                slots_ref[first + x, y], a_ref[x, y, k], preferred_element_type=jnp.float32
-            ).astype(result.dtype)
-
-
-def inner_kernel(codes_hbm, p_hbm, a_hbm, slots_ref, faces, result, codes, p_ref, a_ref, arrived, rows_arrived):
+            for k in range(a_ref.shape[2]):
+                result[x, y, k] = jnp.dot(
+                    slots_ref[first + x, y], a_ref[x, y, k], preferred_element_type=jnp.float32
+                ).astype(result.dtype)
+
+
+def inner_kernel(codes_hbm, p_hbm, a_hbm, slots_ref, result, codes, p_ref, a_ref, arrived, rows_arrived):
     tile_x, slots, unknowns, tile_y, edges = p_ref.shape
     copies = [
         pltpu.make_async_copy(codes_hbm, codes, arrived.at[0]),
@@ -152,7 +150,6 @@
     for copy in copies:
         copy.start()
     row_copies = start_rows(a_hbm, a_ref, rows_arrived, 0)
-    faces[...] = jnp.zeros_like(faces)
     for copy in copies:
         copy.wait()
     pad = pad_rows(unknowns, edges)
@@ -160,15 +157,19 @@
         for m in range(slots):
             p_row = p_ref[x, m]
             for y in range(tile_y):
-                code = codes[m, y, x]
-                block = slot_rows(p_row, m, y, code, pad)
-                faces[x, y, code] = block
-                slots_ref[x, y, m * ROWS : (m + 1) * ROWS, :] = block
+                slots_ref[x, y, m * ROWS : (m + 1) * ROWS, :] = slot_rows(
+                    p_row, m, y, codes[m, y, x], pad
+                )
     finish_rows(row_copies, slots_ref, a_ref, result, 0)
 
 
 def outer_kernel(count_x, unknowns):
-    def body(slots_ref, got_xa, got_xb, a_hbm, result, sides, a_ref, rows_arrived):
+    def body(
+        slots_ref, got_xa, got_xb, codes_hbm, a_hbm,
+        result, sides, faces, codes, a_ref, arrived, rows_arrived,
+    ):
+        copy = pltpu.make_async_copy(codes_hbm, codes, arrived.at[0])
+        copy.start()
         first = a_hbm.shape[0] - a_ref.shape[0]
         row_copies = start_rows(a_hbm, a_ref, rows_arrived, first)
         index, even = place("gx")
@@ -176,6 +177,13 @@
             low, high = x_side(got_xa, got_xb, y, even)
             expand(sides.at[0, y], low, index > 0, unknowns)
             expand(sides.at[1, y], high, index < count_x - 1, unknowns)
+        faces[...] = jnp.zeros_like(faces)
+        copy.wait()
+        for x in range(faces.shape[0]):
+            for y in range(faces.shape[1]):
+                for m in range(codes.shape[0]):
+                    block = slots_ref[x, y, m * ROWS : (m + 1) * ROWS, :]
+                    faces[x, y, codes[m, y, x]] = block
         finish_rows(row_copies, slots_ref, a_ref, result, first)
 
     return body
@@ -204,8 +212,8 @@
 
     def body(
         a_hbm, p_hbm, u_first, u_last, faces, sides, got_ya, got_yb,
-        own, send_xa, send_xb, send_ya, send_yb,
-        a_codes, p_codes, slot_of, part_of, near, products, spread, parts, arrived,
+        parts, send_xa, send_xb, send_ya, send_yb,
+        a_codes, p_codes, slot_of, part_of, near, products, spread, arrived,
     ):
         tile_x, tile_y = faces.shape[:2]
         slots, held, edges = u_first.shape[2:]
@@ -224,10 +232,10 @@
         count = held // ROWS
         for i in range(len(mine)):
             for d in range(9):
-                slot_of[i, d] = slots
+                slot_of[i, d] = len(mine) * slots
             for q in range(5):
                 part_of[i, q] = len(mine) * count
-            products[i, slots] = jnp.zeros(products.shape[2:], products.dtype)
+        products[len(mine) * slots] = jnp.zeros(products.shape[1:], products.dtype)
         parts[len(mine) * count] = jnp.zeros(parts.shape[1:], parts.dtype)
         for y in range(tile_y):
             near[1 + y] = sides[0, y]
@@ -244,20 +252,20 @@
                 low, high = jnp.logical_and(low, inside), jnp.logical_and(high, inside)
             expand(near.at[x * wide], jnp.where(even_y, from_b, from_a), low, unknowns)
             expand(near.at[x * wide + wide - 1], jnp.where(even_y, from_a, from_b), high, unknowns)
-        row = lax.broadcasted_iota(jnp.int32, (held, 128), 0)
-        lane = lax.broadcasted_iota(jnp.int32, (held, 128), 1)
-        picks = jnp.where(jnp.logical_or(lane == row, lane == row + 64), 1.0, 0.0)
-        picks = picks.astype(jnp.bfloat16)
-        wing = lax.broadcasted_iota(jnp.int32, (ROWS, 128), 1) < 64
-        spread[...] = jnp.zeros_like(spread)
+        for o in reversed(range(26)):
+            start = ((o // 5 + 1) * 7 + o % 5 + 1) * unknowns if o < 25 else lanes
+            ended = ((o - 1) // 5 * 7 + 7 + (o - 1) % 5 + 2) * unknowns if o else 0
+            if start > ended:
+                zeros = jnp.zeros((start - ended, spread.shape[2]), spread.dtype)
+                for i in range(spread.shape[0]):
+                    spread[i, ended:start, :] = zeros
         for copy in copies:
             copy.wait()
         for i, (x, y) in enumerate(mine):
             for k in range(slots):
-                slot_of[i, a_codes[x, y, k]] = k
+                slot_of[i, a_codes[x, y, k]] = i * slots + k
             for m in range(1, count):
                 part_of[i, p_codes[m, y, x]] = i * count + m
-        gap = jnp.zeros((64 - held, edges), u_first.dtype)
         for k in range(slots):
             for i, (x, y) in enumerate(mine):
                 code = jnp.minimum(a_codes[x, y, k], 8) if k else 4
@@ -266,15 +274,12 @@
                     step = lax.div(code, 3)
                     spot = (x + step) * wide + y + code - 3 * step
                 one = u_first[x, y, k] if x < half else u_last[x - half, y, k]
-                products[i, k] = lax.dot_general(
-                    near[spot],
-                    jnp.concatenate([one, gap, one, gap], axis=0),
-                    NT,
-                    preferred_element_type=jnp.float32,
+                products[i * slots + k] = lax.dot_general(
+                    near[spot], one, NT, preferred_element_type=jnp.float32
                 )
         for i in range(len(mine)):
             stack = spread.at[i % spread.shape[0]]
-            found = [slot_of[i, d] if d != 4 else 0 for d in range(9)]
+            found = [slot_of[i, d] if d != 4 else i * slots for d in range(9)]
             for o in range(25):
                 value = None
                 for q, (face_x, face_y) in enumerate(face_steps):
@@ -282,30 +287,17 @@
                     if abs(step_x) > 1 or abs(step_y) > 1:
                         continue
                     slot = found[3 * step_x + step_y + 4]
-                    term = products[i, slot, q * ROWS : (q + 1) * ROWS, :]
+                    term = products[slot, q * ROWS : (q + 1) * ROWS, :]
                     value = term if value is None else value + term
+                start = ((o // 5 + 1) * 7 + o % 5 + 1) * unknowns
                 if value is None:
-                    continue
-                high = value.astype(jnp.bfloat16).astype(jnp.float32)
-                start = ((o // 5 + 1) * 7 + o % 5 + 1) * unknowns
-                stack[start : start + unknowns, :] = jnp.where(wing, high, value - high)[:unknowns]
-            terms = lax.dot_general(
-                picks, stack[...].astype(jnp.bfloat16), NT, preferred_element_type=jnp.float32
-            )
+                    value = jnp.zeros((ROWS, held), jnp.float32)
+                stack[start : start + unknowns, :] = value[:unknowns]
+            terms = jnp.transpose(stack[...])
             for m in range(count):
                 parts[i * count + m] = terms[m * ROWS : (m + 1) * ROWS]
 
-        def part(x, y, q):
-            shift = (face_steps[q][0] * 7 + face_steps[q][1]) * unknowns
-            return pltpu.roll(parts[part_of[x * tile_y + y, q]], (-shift) % lanes, 1)
-
-        for i, (x, y) in enumerate(mine):
-            value = parts[i * count]
-            for q in range(1, 5):
-                from_x, from_y = x - face_steps[q][0], y - face_steps[q][1]
-                if 0 <= from_x < tile_x and 0 <= from_y < tile_y:
-                    value += part(from_x, from_y, q)
-            own[x, y] = value[0:unknowns, 0:span]
+        part = part_reader(parts, part_of, tile_y, unknowns)
         for y in range(tile_y):
             low, high = part(0, y, 1), part(tile_x - 1, y, 2)
             send_xa[y] = jnp.where(even_x, high, low).astype(send_xa.dtype)
@@ -316,6 +308,42 @@
             send_yb[x] = jnp.where(even_y, low, high).astype(send_yb.dtype)
 
     return body
+
+
+def part_reader(parts, part_of, tile_y, unknowns):
+    lanes = parts.shape[2]
+
+    def part(x, y, q):
+        shift = (face_steps[q][0] * 7 + face_steps[q][1]) * unknowns
+        return pltpu.roll(parts[part_of[x * tile_y + y, q]], (-shift) % lanes, 1)
+
+    return part
+
+
+def own_kernel(p_hbm, parts, own, p_codes, part_of, arrived):
+    tile_x, tile_y, unknowns, span = own.shape
+    copy = pltpu.make_async_copy(p_hbm, p_codes, arrived.at[0])
+    copy.start()
+    count = p_codes.shape[0]
+    amount = tile_x * tile_y
+    for i in range(amount):
+        for q in range(5):
+            part_of[i, q] = amount * count
+    copy.wait()
+    for x in range(tile_x):
+        for y in range(tile_y):
+            i = x * tile_y + y
+            for m in range(1, count):
+                part_of[i, p_codes[m, y, x]] = i * count + m
+    part = part_reader(parts, part_of, tile_y, unknowns)
+    for x in range(tile_x):
+        for y in range(tile_y):
+            value = parts[(x * tile_y + y) * count]
+            for q in range(1, 5):
+                from_x, from_y = x - face_steps[q][0], y - face_steps[q][1]
+                if 0 <= from_x < tile_x and 0 <= from_y < tile_y:
+                    value += part(from_x, from_y, q)
+            own[x, y] = value[0:unknowns, 0:span]
 
 
 def sum_kernel(count_x, count_y):
@@ -382,13 +410,12 @@
             bytes_accessed=2 * rows * (a_blocks.size // tile_x),
             transcendentals=0,
         )
-        slots_ref, faces, u_first = run(
+        slots_ref, u_first = run(
             inner_kernel,
             (codes, blocks, a_blocks),
             (hbm, hbm, hbm),
             (
                 half(tile_x, tile_y, held * ROWS, edges),
-                half(tile_x, tile_y, 6, ROWS, edges),
                 half(early, tile_y, slots, held * ROWS, edges),
             ),
             scratch=(
@@ -396,7 +423,7 @@
                 pltpu.VMEM(blocks.shape, blocks.dtype),
                 pltpu.VMEM((early, *a_blocks.shape[1:]), a_blocks.dtype),
                 dma((2,)),
-                dma((early, tile_y)),
+                dma((early,)),
             ),
             cost=row_cost(early),
             name="inner",
@@ -410,28 +437,31 @@
         )
         got_ya = lax.ppermute(send_a, AXES, pairs[2])
         got_yb = lax.ppermute(send_b, AXES, pairs[3])
-        u_last, sides = run(
+        u_last, sides, faces = run(
             outer_kernel(count_x, unknowns),
-            (slots_ref, got_xa, got_xb, a_blocks),
-            (inside, inside, inside, hbm),
+            (slots_ref, got_xa, got_xb, codes, a_blocks),
+            (inside, inside, inside, hbm, hbm),
             (
                 half(late, tile_y, slots, held * ROWS, edges),
                 half(2, tile_y, 5 * ROWS, edges),
+                half(tile_x, tile_y, 6, ROWS, edges),
             ),
             scratch=(
+                pltpu.SMEM(codes.shape, codes.dtype),
                 pltpu.VMEM((late, *a_blocks.shape[1:]), a_blocks.dtype),
-                dma((late, tile_y)),
+                dma((1,)),
+                dma((late,)),
             ),
             cost=row_cost(late),
             name="outer",
         )
         amount = tile_x * tile_y
-        own, *sends = run(
+        parts, *sends = run(
             terms_kernel(count_x, count_y, unknowns),
             (a_codes, codes, u_first, u_last, faces, sides, got_ya, got_yb),
             (hbm, hbm) + (inside,) * 6,
             (
-                jax.ShapeDtypeStruct((tile_x, tile_y, unknowns, span), jnp.float32),
+                jax.ShapeDtypeStruct((amount * held + 1, ROWS, lanes), jnp.float32),
                 half(tile_y, ROWS, lanes),
                 half(tile_y, ROWS, lanes),
                 half(tile_x, ROWS, lanes),
@@ -443,14 +473,26 @@
                 pltpu.SMEM((amount, 10), jnp.int32),
                 pltpu.SMEM((amount, 6), jnp.int32),
                 pltpu.VMEM(((tile_x + 2) * (tile_y + 2), 5 * ROWS, edges), jnp.bfloat16),
-                pltpu.VMEM((amount, slots + 1, 5 * ROWS, 128), jnp.float32),
-                pltpu.VMEM((4, lanes, 128), jnp.float32),
-                pltpu.VMEM((amount * held + 1, ROWS, lanes), jnp.float32),
+                pltpu.VMEM((amount * slots + 1, 5 * ROWS, held * ROWS), jnp.float32),
+                pltpu.VMEM((2, lanes, held * ROWS), jnp.float32),
                 dma((2,)),
             ),
             name="terms",
         )
         got = [lax.ppermute(send, AXES, p) for send, p in zip(sends, pairs)]
+        own = run(
+            own_kernel,
+            (codes, parts),
+            (hbm, inside),
+            jax.ShapeDtypeStruct((tile_x, tile_y, unknowns, span), jnp.float32),
+            scratch=(
+                pltpu.SMEM(codes.shape, codes.dtype),
+                pltpu.SMEM((amount, 6), jnp.int32),
+                dma((1,)),
+            ),
+            cost=pl.CostEstimate(flops=0, bytes_accessed=4 << 20, transcendentals=0),
+            name="own",
+        )
         result = run(
             sum_kernel(count_x, count_y),
             (own, *got),

time: 23.4 us -> 22.9 us (0.979)
  starting transfers between devices: 4.57 us -> 4.28 us
    ppermute x4, waiting for transfers between devices: 4.19 us -> 3.48 us  [shards(): got = [lax.ppermute(send, AXES, p) for send, p in zip(sends, pairs)]]
    ppermute x1, waiting for transfers between devices: 0.01 us -> 0.31 us  [shards(): got_xa = lax.ppermute(send_a, AXES, pairs[0])]
    ppermute x4, starting transfers between devices: 2.9 us -> 2.6 us  [shards(): got = [lax.ppermute(send, AXES, p) for send, p in zip(sends, pairs)]]
    pallas_call x6 -> x7, Pallas kernels: 9.32 us -> 9.18 us  [run(): pl.pallas_call(body, out_shape=outputs, in_specs=[pl.BlockSpec(memory_spa...]
  transfers between devices with their start and end apart: 8 -> 8, of which waited for: 4 -> 5; matrix products, arithmetic and copies ran while one was open for 0% -> 0% of each run, Pallas kernels for 20% -> 22%
where the time goes in v5:
time: 22.9 us; the launch traced here: 22.6 us
  Pallas kernels  9.18 us (40%)
  waiting for transfers between devices  9.07 us (40%)
  starting transfers between devices  4.28 us (19%)
    pallas_call x7, Pallas kernels, run(): pl.pallas_call(body, out_shape=outputs, in_specs=[pl.BlockSpec(memory_spa...  9.18 us
    ppermute x4, waiting for transfers between devices, shards(): got = [lax.ppermute(send, AXES, p) for send, p in zip(sends, pairs)]  3.48 us
    ppermute x1, waiting for transfers between devices, shards(): got_yb = lax.ppermute(send_b, AXES, pairs[3])  2.89 us
    ppermute x4, starting transfers between devices, shards(): got = [lax.ppermute(send, AXES, p) for send, p in zip(sends, pairs)]  2.6 us
    ppermute x1, waiting for transfers between devices, shards(): got_xb = lax.ppermute(send_b, AXES, pairs[1])  2.39 us
    ppermute x1, starting transfers between devices, shards(): got_xa = lax.ppermute(send_a, AXES, pairs[0])  1.56 us
  transfers between devices with their start and end apart: 8, of which 5 were waited for; matrix products, arithmetic and copies ran while one was open for 0% of the time, Pallas kernels for 22%

profile of v5, /device:TPU:4, one launch (start us, length us, event | category | flops | bytes accessed | tf_op | source)
XLA Modules:
  0.0 22.6 jit_solution(14336900535214941803)
XLA Ops:
  0.0 1.0 %edges.1 = (bf16[1,3,48,128]{3,2,1,0:T(8,128)(2,1)S(1)}, bf16[1,3,48,128]{3,2,1,0:T(8,128)(2,1)S(1)}) custom-call(s32[3,2,4]{2,1,0:T(2,128)} %bitcast.5, bf16[4,3,12,2,192]{4,3,2,1,0:T(2,128)(2,1)} %bitcast.3), custom_call_target="tpu_custom_call" | custom-call | tf_op jit(solution)/shard_map/edges/pallas_call | solution.py:49
  1.0 1.6 %collective-permute-start = (bf16[1,3,48,128]{3,2,1,0:T(8,128)(2,1)S(1)}, bf16[1,3,48,128]{3,2,1,0:T(8,128)(2,1)S(1)}, u32[]{:S(2)}, u32[]{:S(2)}) collective-permute-start(bf16[1,3,48,128]{3,2,1,0:T(8,128)(2,1)S(1)} %get-tuple-element.21), channel_id=1, source_target_pairs={{0,8},{1,9},{2,10},{3,11},{4,12},{5,13},{6,14},{7,15},{8,0},{9,1},... | collective-permute-start | bytes 110600 | tf_op jit(solution)/shard_map/ppermute | solution.py:404
  2.6 0.0 collective-permute-start.1
  2.6 2.1 %inner.1 = (bf16[4,2,48,192]{3,2,1,0:T(8,128)(2,1)S(1)}, bf16[2,2,5,48,192]{4,3,2,1,0:T(8,128)(2,1)S(1)}) custom-call(s32[3,2,4]{2,1,0:T(2,128)} %bitcast.6, bf16[4,3,12,2,192]{4,3,2,1,0:T(2,128)(2,1)} %bitcast.4, bf16[4,2,5,192,192]{4,3,2,1,0:T(8,128)(2,1)} %a_hbm.4), custom_call_target="tpu_custom_call" | custom-call | flops 70778880 | bytes 1474560 | tf_op jit(solution)/shard_map/inner/pallas_call | solution.py:49
  4.7 0.3 %collective-permute-done.got_xa.got_a = bf16[1,3,48,128]{3,2,1,0:T(8,128)(2,1)S(1)} collective-permute-done((bf16[1,3,48,128]{3,2,1,0:T(8,128)(2,1)S(1)}, bf16[1,3,48,128]{3,2,1,0:T(8,128)(2,1)S(1)}, u32[]{:S(2)}, u32[]{:S(2)}) %collective-permute-start) | collective-permute-done | bytes 36896 | tf_op jit(solution)/shard_map/ppermute | solution.py:404
  5.0 2.4 %collective-permute-done.1.got_xb.got_b = bf16[1,3,48,128]{3,2,1,0:T(8,128)(2,1)S(1)} collective-permute-done((bf16[1,3,48,128]{3,2,1,0:T(8,128)(2,1)S(1)}, bf16[1,3,48,128]{3,2,1,0:T(8,128)(2,1)S(1)}, u32[]{:S(2)}, u32[]{:S(2)}) %collective-permute-start.1) | collective-permute-done | bytes 36896 | tf_op jit(solution)/shard_map/ppermute | solution.py:405
  7.4 0.1 strips.1
  7.6 0.0 collective-permute-start.2
  7.6 0.1 collective-permute-start.3
  7.7 1.8 %outer.1 = (bf16[2,2,5,48,192]{4,3,2,1,0:T(8,128)(2,1)S(1)}, bf16[2,2,80,192]{3,2,1,0:T(8,128)(2,1)S(1)}, bf16[4,2,6,16,192]{4,3,2,1,0:T(8,128)(2,1)S(1)}) custom-call(bf16[4,2,48,192]{3,2,1,0:T(8,128)(2,1)S(1)} %get-tuple-element.20.slots_ref, bf16[1,3,48,128]{3,2,1,0:T(8,128)(2,1)S(1)} %collective-permute-done.got_xa.got_a, ...), custom_call_target="tpu_custom_call" | custom-call | flops 70778880 | bytes 1474560 | tf_op jit(solution)/shard_map/outer/pallas_call | solution.py:49
  9.5 0.0 collective-permute-done.2.got_ya
  9.5 2.9 %collective-permute-done.3.got_yb = bf16[3,3,48,128]{3,2,1,0:T(8,128)(2,1)S(1)} collective-permute-done((bf16[3,3,48,128]{3,2,1,0:T(8,128)(2,1)S(1)}, bf16[3,3,48,128]{3,2,1,0:T(8,128)(2,1)S(1)}, u32[]{:S(2)}, u32[]{:S(2)}) %collective-permute-start.3) | collective-permute-done | bytes 110624 | tf_op jit(solution)/shard_map/ppermute | solution.py:439
  12.4 2.2 %terms.1 = (f32[25,16,640]{2,1,0:T(8,128)S(1)}, bf16[2,16,640]{2,1,0:T(8,128)(2,1)S(1)}, bf16[2,16,640]{2,1,0:T(8,128)(2,1)S(1)}, bf16[4,16,640]{2,1,0:T(8,128)(2,1)S(1)}, bf16[4,16,640]{2,1,0:T(8,128)(2,1)S(1)}) custom-call(s32[4,2,5]{2,1,0:T(2,128)} %a_hbm.5, s32[3,2,4]{2,1,0:T(2,128)} %bitcast.8, ...), custom_call_target="tpu_custom_call" | custom-call | tf_op jit(solution)/shard_map/terms/pallas_call | solution.py:49
  14.6 0.2 collective-permute-start.6
  14.8 0.0 collective-permute-start.7
  14.8 2.0 %collective-permute-start.4 = (bf16[2,16,640]{2,1,0:T(8,128)(2,1)S(1)}, bf16[2,16,640]{2,1,0:T(8,128)(2,1)S(1)}, u32[]{:S(2)}, u32[]{:S(2)}) collective-permute-start(bf16[2,16,640]{2,1,0:T(8,128)(2,1)S(1)} %get-tuple-element.29), channel_id=1, source_target_pairs={{0,8},{1,9},{2,10},{3,11},{4,12},{5,13},{6,14},{7,15},{8,0},{9,1},... | collective-permute-start | bytes 122888 | tf_op jit(solution)/shard_map/ppermute | solution.py:482
  16.9 0.4 %collective-permute-start.5 = (bf16[2,16,640]{2,1,0:T(8,128)(2,1)S(1)}, bf16[2,16,640]{2,1,0:T(8,128)(2,1)S(1)}, u32[]{:S(2)}, u32[]{:S(2)}) collective-permute-start(bf16[2,16,640]{2,1,0:T(8,128)(2,1)S(1)} %get-tuple-element.30), channel_id=1, source_target_pairs={{0,1},{1,0},{2,3},{3,2},{4,5},{5,4},{6,7},{7,6},{8,16},{9,17},{10,... | collective-permute-start | bytes 122888 | tf_op jit(solution)/shard_map/ppermute | solution.py:482
  17.2 1.0 %own.1 = f32[4,2,12,588]{3,2,1,0:T(8,128)S(1)} custom-call(s32[3,2,4]{2,1,0:T(2,128)} %bitcast.9, f32[25,16,640]{2,1,0:T(8,128)S(1)} %get-tuple-element.28.parts), custom_call_target="tpu_custom_call" | custom-call | bytes 4194304 | tf_op jit(solution)/shard_map/own/pallas_call | solution.py:49
  18.3 1.9 %collective-permute-done.4.got_xa = bf16[2,16,640]{2,1,0:T(8,128)(2,1)S(1)} collective-permute-done((bf16[2,16,640]{2,1,0:T(8,128)(2,1)S(1)}, bf16[2,16,640]{2,1,0:T(8,128)(2,1)S(1)}, u32[]{:S(2)}, u32[]{:S(2)}) %collective-permute-start.4) | collective-permute-done | bytes 40992 | tf_op jit(solution)/shard_map/ppermute | solution.py:482
  20.2 1.6 %collective-permute-done.5.got_xb = bf16[2,16,640]{2,1,0:T(8,128)(2,1)S(1)} collective-permute-done((bf16[2,16,640]{2,1,0:T(8,128)(2,1)S(1)}, bf16[2,16,640]{2,1,0:T(8,128)(2,1)S(1)}, u32[]{:S(2)}, u32[]{:S(2)}) %collective-permute-start.5) | collective-permute-done | bytes 40992 | tf_op jit(solution)/shard_map/ppermute | solution.py:482
  21.8 0.0 collective-permute-done.6.got_ya
  21.8 0.0 collective-permute-done.7.got_yb
  21.8 0.8 %sum.1 = f32[4,12,2,588]{3,2,1,0:T(2,128)} custom-call(f32[4,2,12,588]{3,2,1,0:T(8,128)S(1)} %own.1, bf16[2,16,640]{2,1,0:T(8,128)(2,1)S(1)} %collective-permute-done.4.got_xa, bf16[2,16,640]{2,1,0:T(8,128)(2,1)S(1)} %collective-permute-done.5.got_xb, bf16[4,16,640]{2,1,0:T(8,128)(2,1)S(1)} %collective-permute-done.6.got_ya, ...), custom_call_target="tpu_custom_call" | custom-call | tf_op jit(solution)/shard_map/sum/pallas_call | solution.py:49
Async XLA Ops:
  1.0 4.0 %collective-permute-start = (bf16[1,3,48,128]{3,2,1,0:T(8,128)(2,1)S(1)}, bf16[1,3,48,128]{3,2,1,0:T(8,128)(2,1)S(1)}, u32[]{:S(2)}, u32[]{:S(2)}) collective-permute-start(bf16[1,3,48,128]{3,2,1,0:T(8,128)(2,1)S(1)} %get-tuple-element.21), channel_id=1, source_target_pairs={{0,8},{1,9},{2,10},{3,11},{4,12},{5,13},{6,14},{7,15},{8,0},{9,1},... | collective-permute-start | bytes 110600 | tf_op jit(solution)/shard_map/ppermute | solution.py:404
  2.6 4.9 %collective-permute-start.1 = (bf16[1,3,48,128]{3,2,1,0:T(8,128)(2,1)S(1)}, bf16[1,3,48,128]{3,2,1,0:T(8,128)(2,1)S(1)}, u32[]{:S(2)}, u32[]{:S(2)}) collective-permute-start(bf16[1,3,48,128]{3,2,1,0:T(8,128)(2,1)S(1)} %get-tuple-element.22), channel_id=1, source_target_pairs={{0,1},{1,0},{2,3},{3,2},{4,5},{5,4},{6,7},{7,6},{8,16},{9,17},{10,... | collective-permute-start | bytes 110600 | tf_op jit(solution)/shard_map/ppermute | solution.py:405
  7.6 2.0 %collective-permute-start.2 = (bf16[3,3,48,128]{3,2,1,0:T(8,128)(2,1)S(1)}, bf16[3,3,48,128]{3,2,1,0:T(8,128)(2,1)S(1)}, u32[]{:S(2)}, u32[]{:S(2)}) collective-permute-start(bf16[3,3,48,128]{3,2,1,0:T(8,128)(2,1)S(1)} %get-tuple-element.26), channel_id=1, source_target_pairs={{0,1},{8,9},{16,17},{24,25},{1,0},{9,8},{17,16},{25,24},{2,3},{10,... | collective-permute-start | bytes 331784 | tf_op jit(solution)/shard_map/ppermute | solution.py:438
  7.6 4.8 %collective-permute-start.3 = (bf16[3,3,48,128]{3,2,1,0:T(8,128)(2,1)S(1)}, bf16[3,3,48,128]{3,2,1,0:T(8,128)(2,1)S(1)}, u32[]{:S(2)}, u32[]{:S(2)}) collective-permute-start(bf16[3,3,48,128]{3,2,1,0:T(8,128)(2,1)S(1)} %get-tuple-element.27), channel_id=1, source_target_pairs={{0,8},{8,0},{16,24},{24,16},{1,2},{9,10},{17,18},{25,26},{2,1},{10... | collective-permute-start | bytes 331784 | tf_op jit(solution)/shard_map/ppermute | solution.py:439
  14.6 7.1 %collective-permute-start.6 = (bf16[4,16,640]{2,1,0:T(8,128)(2,1)S(1)}, bf16[4,16,640]{2,1,0:T(8,128)(2,1)S(1)}, u32[]{:S(2)}, u32[]{:S(2)}) collective-permute-start(bf16[4,16,640]{2,1,0:T(8,128)(2,1)S(1)} %get-tuple-element.31), channel_id=1, source_target_pairs={{0,1},{8,9},{16,17},{24,25},{1,0},{9,8},{17,16},{25,24},{2,3},{10,... | collective-permute-start | bytes 245768 | tf_op jit(solution)/shard_map/ppermute | solution.py:482
  14.8 6.9 %collective-permute-start.7 = (bf16[4,16,640]{2,1,0:T(8,128)(2,1)S(1)}, bf16[4,16,640]{2,1,0:T(8,128)(2,1)S(1)}, u32[]{:S(2)}, u32[]{:S(2)}) collective-permute-start(bf16[4,16,640]{2,1,0:T(8,128)(2,1)S(1)} %get-tuple-element.32), channel_id=1, source_target_pairs={{0,8},{8,0},{16,24},{24,16},{1,2},{9,10},{17,18},{25,26},{2,1},{10... | collective-permute-start | bytes 245768 | tf_op jit(solution)/shard_map/ppermute | solution.py:482
  14.8 5.3 %collective-permute-start.4 = (bf16[2,16,640]{2,1,0:T(8,128)(2,1)S(1)}, bf16[2,16,640]{2,1,0:T(8,128)(2,1)S(1)}, u32[]{:S(2)}, u32[]{:S(2)}) collective-permute-start(bf16[2,16,640]{2,1,0:T(8,128)(2,1)S(1)} %get-tuple-element.29), channel_id=1, source_target_pairs={{0,8},{1,9},{2,10},{3,11},{4,12},{5,13},{6,14},{7,15},{8,0},{9,1},... | collective-permute-start | bytes 122888 | tf_op jit(solution)/shard_map/ppermute | solution.py:482
  16.9 4.9 %collective-permute-start.5 = (bf16[2,16,640]{2,1,0:T(8,128)(2,1)S(1)}, bf16[2,16,640]{2,1,0:T(8,128)(2,1)S(1)}, u32[]{:S(2)}, u32[]{:S(2)}) collective-permute-start(bf16[2,16,640]{2,1,0:T(8,128)(2,1)S(1)} %get-tuple-element.30), channel_id=1, source_target_pairs={{0,1},{1,0},{2,3},{3,2},{4,5},{5,4},{6,7},{7,6},{8,16},{9,17},{10,... | collective-permute-start | bytes 122888 | tf_op jit(solution)/shard_map/ppermute | solution.py:482
